TPU v7x, 128 devices: a whole 4x4x4 slice. The times are simulated.
128 devices in a mesh: head: 8 (over x, y_hi), ctx: 16 (over y_lo, z, core).
Axes of the slice: x: 4, y: 4 (y_hi: 2, y_lo: 2; y = y_hi * 2 + y_lo), z: 4, core: 2. Of those that a mesh axis runs over, the one named last changes fastest.
Arguments:
- main_query: bfloat16 [2048, 73728], P('ctx', 'head'), may hold values from -400 to 400
- latent: bfloat16 [131072, 576], P('ctx'), may hold values from -20 to 20
- index_query: bfloat16 [2048, 8192], P('ctx', 'head'), may hold values from -400 to 400
- index_key: bfloat16 [131072, 128], P('ctx'), may hold values from -20 to 20
- index_weight: float32 [2048, 64], P('ctx', 'head'), may hold values from -0.1 to 0.1
- selected: int32 [2048, 32], P('ctx'), may hold values from 0 to 2047, as said below
- lengths: int32 [2048], P('ctx'), may hold values from 1985 to 131072
- cotangent: float32 [2048], P('ctx'), may hold values from 64 to 512
Outputs:
- index_query_grad: float32 [2048, 8192], P('ctx', 'head')
- index_weight_grad: float32 [2048, 64], P('ctx', 'head')
- index_key_grad: float32 [131072, 128], P('ctx')
Inputs may be any that keep to these rules, and one draw needn't show every extreme that they name: `selected`: each query names 32 distinct blocks in rising order, all holding at least one visible token; its last block holds its last visible token and all others are fully visible. The queries of one ctx index name exactly 64 distinct blocks in all, at most 8 of them among the tokens of any one ctx index, and exactly 8 among those of ctx index 0.
All inputs are finite; a program needn't handle non-finite values.
Results may differ from a plain program's by a relative error of at most 0.0026.
Values may be sent and summed in bfloat16 or wider, within the bound.
A program may use at most 128 MiB of HBM per device.

v0:
```python
import jax
import jax.numpy as jnp
from jax import lax
from jax.sharding import PartitionSpec as P

HEADS = 128
BLK = 64
POOL = 64
MOST = 8


logit_scale = 192.0 ** (-0.5)


def masked_softmax(values, visible):
    highest = jnp.max(jnp.where(visible, values, -jnp.inf), axis=-1, keepdims=True)
    weights = jnp.where(visible, jnp.exp(values - highest), 0.0)
    return weights / jnp.sum(weights, axis=-1, keepdims=True)


def row_product(left, right):
    return lax.dot_general(
        left, right, (((1,), (1,)), ((), ())), preferred_element_type=jnp.float32
    )


def shards(main_query, latent, index_query, index_key, index_weight, selected, lengths, cotangent):
    ctx_count = lax.axis_size("ctx")
    token_rows = latent.shape[0]
    latent_width = latent.shape[1]
    index_width = index_key.shape[1]
    blocks_each = token_rows // BLK
    block_total = ctx_count * blocks_each
    query_count = main_query.shape[0]
    main_heads = main_query.shape[1] // latent_width
    index_heads = index_weight.shape[1]
    union_rows = POOL * BLK
    block_numbers = jnp.arange(block_total, dtype=jnp.int32)
    present = jnp.any(selected.reshape(-1)[:, None] == block_numbers[None, :], axis=0)
    present_int = present.astype(jnp.int32)
    position = jnp.cumsum(present_int) - 1
    owner_rank = jnp.cumsum(present_int.reshape(ctx_count, blocks_each), axis=1) - 1
    union_index = jnp.arange(POOL, dtype=jnp.int32)
    block_ids = jnp.sum(
        jnp.where(
            present[None, :] & (position[None, :] == union_index[:, None]),
            block_numbers[None, :],
            0,
        ),
        axis=1,
    )
    source_slot = jnp.maximum(
        block_ids // blocks_each * MOST + owner_rank.reshape(-1)[block_ids], 0
    )
    local_ids = jnp.arange(blocks_each, dtype=jnp.int32)
    slot_numbers = jnp.arange(MOST, dtype=jnp.int32)
    requests = jnp.sum(
        jnp.where(
            present.reshape(ctx_count, blocks_each)[:, None, :]
            & (owner_rank[:, None, :] == slot_numbers[None, :, None]),
            local_ids[None, None, :],
            0,
        ),
        axis=2,
    )
    asked_blocks = lax.all_to_all(requests, "ctx", split_axis=0, concat_axis=0, tiled=True)
    latent_blocks = latent.reshape(blocks_each, BLK, latent_width)
    index_blocks = index_key.reshape(blocks_each, BLK, index_width)
    fetched_latent, fetched_index = (
        lax.all_to_all(latent_blocks[asked_blocks], "ctx", split_axis=0, concat_axis=0, tiled=True),
        lax.all_to_all(index_blocks[asked_blocks], "ctx", split_axis=0, concat_axis=0, tiled=True),
    )
    union_latent = fetched_latent.reshape(ctx_count * MOST, BLK, latent_width)[source_slot].reshape(
        union_rows, latent_width
    )
    union_index_key = fetched_index.reshape(ctx_count * MOST, BLK, index_width)[
        source_slot
    ].reshape(union_rows, index_width)
    slot_of_query = position[selected]
    member = jnp.any(slot_of_query[:, :, None] == union_index[None, None, :], axis=1)
    union_tokens = (block_ids[:, None] * BLK + jnp.arange(BLK, dtype=jnp.int32)[None, :]).reshape(
        -1
    )
    visible = jnp.repeat(member, BLK, axis=1) & (union_tokens[None, :] < lengths[:, None])
    step_rows = min(32, query_count)
    step_count = query_count // step_rows

    def blocked(array):
        return array.reshape((step_count, step_rows) + array.shape[1:])

    def forward_block(operands):
        query_block, indexer_block, weight_block, visible_block = operands
        score_matrix = row_product(
            query_block.reshape(step_rows * main_heads, latent_width), union_latent
        )
        score_matrix = score_matrix.reshape(step_rows, main_heads, union_rows) * logit_scale
        head_total = jnp.sum(masked_softmax(score_matrix, visible_block[:, None, :]), axis=1)
        raw_logits = row_product(
            indexer_block.reshape(step_rows * index_heads, index_width), union_index_key
        )
        raw_logits = raw_logits.reshape(step_rows, index_heads, union_rows)
        partial_scores = jnp.sum(weight_block[:, :, None] * jnp.maximum(raw_logits, 0.0), axis=1)
        return (head_total, partial_scores, raw_logits)

    head_total, partial_scores, stored_pre = lax.map(
        forward_block,
        (blocked(main_query), blocked(index_query), blocked(index_weight), blocked(visible)),
    )
    head_total = head_total.reshape(query_count, union_rows)
    partial_scores = partial_scores.reshape(query_count, union_rows)
    summed_probs, index_scores = lax.psum((head_total, partial_scores), "head")
    target = summed_probs / HEADS
    chosen = masked_softmax(index_scores, visible)
    grad_scores = cotangent[:, None] * (chosen - target)

    def backward_block(running, operands):
        indexer_block, weight_block, grad_block, raw_logits = operands
        weight_grad = jnp.sum(jnp.maximum(raw_logits, 0.0) * grad_block[:, None, :], axis=2)
        link_weights = jnp.where(
            raw_logits > 0, grad_block[:, None, :] * weight_block[:, :, None], 0.0
        ).astype(jnp.bfloat16)
        link_weights = link_weights.reshape(step_rows * index_heads, union_rows)
        query_gradient = jnp.dot(
            link_weights, union_index_key, preferred_element_type=jnp.float32
        ).reshape(step_rows, index_heads * index_width)
        running = running + lax.dot_general(
            link_weights,
            indexer_block.reshape(step_rows * index_heads, index_width),
            (((0,), (0,)), ((), ())),
            preferred_element_type=jnp.float32,
        )
        return (running, (query_gradient, weight_grad))

    union_grad, (query_gradient, weight_grad) = lax.scan(
        backward_block,
        jnp.zeros((union_rows, index_width), jnp.float32),
        (blocked(index_query), blocked(index_weight), blocked(grad_scores), stored_pre),
    )
    padded = (
        jnp.zeros((ctx_count * MOST, BLK, index_width), jnp.float32)
        .at[source_slot]
        .add(union_grad.reshape(POOL, BLK, index_width))
    )
    padded = padded.reshape(ctx_count, MOST, BLK, index_width)
    returned = lax.all_to_all(padded, "ctx", split_axis=0, concat_axis=0, tiled=True)
    owned_grad = (
        jnp.zeros((blocks_each, BLK, index_width), jnp.float32)
        .at[asked_blocks.reshape(-1)]
        .add(returned.reshape(ctx_count * MOST, BLK, index_width))
    )
    key_grad = lax.psum(owned_grad.reshape(token_rows, index_width), "head")
    return (
        query_gradient.reshape(query_count, index_heads * index_width),
        weight_grad.reshape(query_count, index_heads),
        key_grad,
    )


def solution(mesh):
    return jax.shard_map(
        shards,
        mesh=mesh,
        in_specs=(
            P("ctx", "head"),
            P("ctx", None),
            P("ctx", "head"),
            P("ctx", None),
            P("ctx", "head"),
            P("ctx", None),
            P("ctx"),
            P("ctx"),
        ),
        out_specs=(P("ctx", "head"), P("ctx", "head"), P("ctx", None)),
        check_vma=False,
    )
```

profile of v0, /device:TPU:0, one launch (start us, length us, event | category | flops | bytes accessed | tf_op | source)
XLA Modules:
  0.0 957.7 jit_solution(10510666388499681511)
XLA Ops:
  8.2 5.6 fusion.36
  14.7 12.4 %all_to_all.27 = s32[16,1,8]{2,1,0:T(1,128)S(1)} all-to-all(s32[16,1,8]{2,1,0:T(1,128)S(1)} %bitcast.164), channel_id=1, replica_groups=mesh['head'=8,'ctx'=16] {'ctx'}, dimensions={0} | all-to-all | bytes 1024 | tf_op jit(solution)/shard_map/all_to_all | solution.py:66
  27.8 2.1 gather_fusion.4
  29.9 3.7 all-to-all-start.2
  33.7 14.1 %copy.56 = bf16[8192,576]{1,0:T(8,128)(2,1)} copy(bf16[8192,576]{0,1:T(8,128)(2,1)} %param.13) | data formatting | bytes 18874368 | tf_op args[1]
  47.8 11.8 %gather_fusion.1 = bf16[128,64,576]{2,1,0:T(8,128)(2,1)} fusion(bf16[128,64,576]{2,1,0:T(8,128)(2,1)} %bitcast.148, s32[1024]{0:T(1024)S(1)} %pad_clamp_fusion.2), kind=kCustom, calls=%fused_computation.1 | custom fusion | bytes 18874880 | tf_op jit(solution)/shard_map/gather | solution.py:70
  59.6 2.9 all-to-all-done.2
  62.5 5.4 all-to-all-start.1
  68.7 23.0 %gather_fusion = s32[4096]{0:T(1024)S(1)} fusion(s32[2048]{0:T(1024)S(1)} %get-tuple-element.239, s32[4096]{0:T(1024)S(1)} %broadcast_clamp_fusion), kind=kCustom, calls=%fused_computation | custom fusion | bytes 49152 | tf_op jit(solution)/shard_map/gather | solution.py:79
  92.2 2.8 broadcast_in_dim.125.clone
  94.9 2.5 reshape.322
  98.5 2.3 compare_and_fusion
  101.5 123.1 %all-to-all-done.1 = bf16[16,8,64,576]{3,2,1,0:T(8,128)(2,1)} async-done(((bf16[16,8,64,576]{3,2,1,0:T(8,128)(2,1)}), bf16[16,8,64,576]{3,2,1,0:T(8,128)(2,1)}, u32[]{:S(2)}, u32[]{:S(2)}) %all-to-all-start.1) | async-done | bytes 9437216 | tf_op jit(solution)/shard_map/all_to_all | solution.py:70
  224.7 7.5 gather_fusion.3
  232.2 7.7 copy.62
  239.9 162.8 %while.29 = (s32[]{:T(128)}, f32[4,32,4096]{2,1,0:T(8,128)}, f32[4,32,4096]{2,1,0:T(8,128)}, f32[4,32,8,4096]{3,2,1,0:T(8,128)}, pred[4,32,4096]{2,1,0:T(8,128)(...) while((s32[]{:T(128)}, f32[4,32,4096]{2,1,0:T(8,128)}, ...), condition=%wide.region_11.12_spmd, body=%wide.region_6.11_spmd.sunk | while | flops 2712417792 | bytes 67244160 | solution.py:105
  241.5 7.9 fusion.71
  250.4 12.7 %fusion.72 = f32[32,16,4096]{2,1,0:T(8,128)} fusion(f32[32,16,4096]{2,1,0:T(8,128)} %fusion.71, pred[32,4096]{1,0:T(8,128)(4,1)S(1)} %dynamic-slice_bitcast_fusion.7), kind=kOutput, calls=%fused_computation.8.clone.1 | output fusion | flops 10494974 | bytes 16908288 | tf_op jit(solution)/shard_map/while/body/eval_jaxpr/div | solution.py:18
  263.1 12.5 %divide_reduce_fusion.2 = f32[32,4096]{1,0:T(8,128)S(1)} fusion(f32[32,16,4096]{2,1,0:T(8,128)} %fusion.72, f32[32,16,4096]{2,1,0:T(8,128)} %fusion.71, pred[32,4096]{1,0:T(8,128)(4,1)S(1)} %dynamic-slice_bitcast_fusion.7), kind=kOutput, calls=%fused_computation.13.clone.1 | output fusion | flops 14553599 | bytes 17432576 | tf_op jit(solution)/shard_map/while/body/eval_jaxpr/sub | solution.py:17
  275.7 1.6 fusion.70
  278.3 2.2 bitcast_dynamic-update-slice_fusion.8
  282.2 7.9 fusion.71
  291.0 12.7 %fusion.72 = f32[32,16,4096]{2,1,0:T(8,128)} fusion(f32[32,16,4096]{2,1,0:T(8,128)} %fusion.71, pred[32,4096]{1,0:T(8,128)(4,1)S(1)} %dynamic-slice_bitcast_fusion.7), kind=kOutput, calls=%fused_computation.8.clone.1 | output fusion | flops 10494974 | bytes 16908288 | tf_op jit(solution)/shard_map/while/body/eval_jaxpr/div | solution.py:18
  303.8 12.5 %divide_reduce_fusion.2 = f32[32,4096]{1,0:T(8,128)S(1)} fusion(f32[32,16,4096]{2,1,0:T(8,128)} %fusion.72, f32[32,16,4096]{2,1,0:T(8,128)} %fusion.71, pred[32,4096]{1,0:T(8,128)(4,1)S(1)} %dynamic-slice_bitcast_fusion.7), kind=kOutput, calls=%fused_computation.13.clone.1 | output fusion | flops 14553599 | bytes 17432576 | tf_op jit(solution)/shard_map/while/body/eval_jaxpr/sub | solution.py:17
  316.4 1.6 fusion.70
  319.0 2.3 bitcast_dynamic-update-slice_fusion.8
  322.9 7.9 fusion.71
  331.7 12.7 %fusion.72 = f32[32,16,4096]{2,1,0:T(8,128)} fusion(f32[32,16,4096]{2,1,0:T(8,128)} %fusion.71, pred[32,4096]{1,0:T(8,128)(4,1)S(1)} %dynamic-slice_bitcast_fusion.7), kind=kOutput, calls=%fused_computation.8.clone.1 | output fusion | flops 10494974 | bytes 16908288 | tf_op jit(solution)/shard_map/while/body/eval_jaxpr/div | solution.py:18
  344.5 12.5 %divide_reduce_fusion.2 = f32[32,4096]{1,0:T(8,128)S(1)} fusion(f32[32,16,4096]{2,1,0:T(8,128)} %fusion.72, f32[32,16,4096]{2,1,0:T(8,128)} %fusion.71, pred[32,4096]{1,0:T(8,128)(4,1)S(1)} %dynamic-slice_bitcast_fusion.7), kind=kOutput, calls=%fused_computation.13.clone.1 | output fusion | flops 14553599 | bytes 17432576 | tf_op jit(solution)/shard_map/while/body/eval_jaxpr/sub | solution.py:17
  357.1 1.6 fusion.70
  359.7 2.3 bitcast_dynamic-update-slice_fusion.8
  363.6 7.9 fusion.71
  372.5 12.7 %fusion.72 = f32[32,16,4096]{2,1,0:T(8,128)} fusion(f32[32,16,4096]{2,1,0:T(8,128)} %fusion.71, pred[32,4096]{1,0:T(8,128)(4,1)S(1)} %dynamic-slice_bitcast_fusion.7), kind=kOutput, calls=%fused_computation.8.clone.1 | output fusion | flops 10494974 | bytes 16908288 | tf_op jit(solution)/shard_map/while/body/eval_jaxpr/div | solution.py:18
  385.2 12.5 %divide_reduce_fusion.2 = f32[32,4096]{1,0:T(8,128)S(1)} fusion(f32[32,16,4096]{2,1,0:T(8,128)} %fusion.72, f32[32,16,4096]{2,1,0:T(8,128)} %fusion.71, pred[32,4096]{1,0:T(8,128)(4,1)S(1)} %dynamic-slice_bitcast_fusion.7), kind=kOutput, calls=%fused_computation.13.clone.1 | output fusion | flops 14553599 | bytes 17432576 | tf_op jit(solution)/shard_map/while/body/eval_jaxpr/sub | solution.py:17
  397.8 1.6 fusion.70
  400.4 2.2 bitcast_dynamic-update-slice_fusion.8
  402.7 3.1 copy.63
  405.8 1.8 copy.64
  407.6 192.3 %all-reduce.6.cloned.1.call-done = (f32[128,4096]{0,1:T(8,128)}, f32[128,4096]{0,1:T(8,128)}) async-done(((f32[128,4096]{0,1:T(8,128)}, f32[128,4096]{0,1:T(8,128)}), (f32[128,4096]{0,1:T(8,128)}, f32[128,4096]{0,1:T(8,128)})) %all-reduce.6.cloned.1.call-update) | async-done | bytes 4194320 | tf_op jit(solution)/shard_map/psum | solution.py:111
  599.9 2.1 select_reduce_fusion.1
  602.0 2.0 fusion.37
  604.0 2.2 subtract_multiply_fusion
  606.2 3.0 copy.65
  609.1 48.4 %while.30 = (s32[]{:T(128)}, f32[4096,128]{1,0:T(8,128)}, f32[4,32,1024]{2,1,0:T(8,128)}, f32[4,32,8]{2,1,0:T(8,128)S(1)}, f32[4,32,8,4096]{3,2,1,0:T(8,128)}, /...) while((s32[]{:T(128)}, f32[4096,128]{1,0:T(8,128)}, ...), condition=%wide.region_18.19_spmd.clone, body=%wide.region_16.18_spmd.clone.sunk | while | flops 548404992 | bytes 20453004 | solution.py:134
  610.2 2.7 fusion.77
  612.9 2.8 dynamic-slice_compare_fusion.2
  615.8 2.5 convolution_add_fusion.2
  621.1 2.7 fusion.77
  623.8 2.8 dynamic-slice_compare_fusion.2
  626.7 4.1 convolution_add_fusion.2
  633.6 2.7 fusion.77
  636.3 2.8 dynamic-slice_compare_fusion.2
  639.2 4.1 convolution_add_fusion.2
  646.1 2.7 fusion.77
  648.8 2.8 dynamic-slice_compare_fusion.2
  651.7 4.1 convolution_add_fusion.2
  657.5 2.5 broadcast.212.clone
  660.1 9.0 scatter_fusion
  669.1 5.3 all-to-all-start.3
  675.7 54.9 %all-to-all-done.3 = f32[16,8,64,128]{3,2,1,0:T(8,128)} async-done(((f32[16,8,64,128]{3,2,1,0:T(8,128)}), f32[16,8,64,128]{3,2,1,0:T(8,128)}, u32[]{:S(2)}, u32[]{:S(2)}) %all-to-all-start.3) | async-done | bytes 4194336 | tf_op jit(solution)/shard_map/all_to_all | solution.py:145
  730.6 2.5 broadcast.212
  733.1 20.1 %scatter_fusion.1 = f32[128,64,128]{2,1,0:T(8,128)} fusion(f32[128,64,128]{2,1,0:T(8,128)} %broadcast.212, s32[128]{0:T(128)S(1)} %fusion.42, f32[128,64,128]{2,1,0:T(8,128)} %bitcast.36), kind=kCustom, calls=%fused_computation.7 | custom fusion | flops 1048576 | bytes 12583424 | tf_op jit(solution)/shard_map/scatter-add | solution.py:149
  753.9 192.4 %all-reduce.4.cloned.1.call-done = f32[8192,128]{1,0:T(8,128)} async-done(((f32[8192,128]{1,0:T(8,128)}), f32[8192,128]{1,0:T(8,128)}) %all-reduce.4.cloned.1.call-update) | async-done | bytes 4194320 | tf_op jit(solution)/shard_map/psum | solution.py:151
  946.3 4.6 copy.105
  (141 shorter events, 33.6 us)
Async XLA Ops:
  7.2 20.6 %copy-start = (bf16[8192,128]{1,0:T(8,128)(2,1)S(1)}, bf16[8192,128]{1,0:T(8,128)(2,1)}, u32[]{:S(2)}) copy-start(bf16[8192,128]{1,0:T(8,128)(2,1)} %param.15) | copy-start | bytes 6291460
  27.1 0.6 copy-start.7
  29.9 32.5 %all-to-all-start.2 = ((bf16[16,8,64,128]{3,2,1,0:T(8,128)(2,1)}), bf16[16,8,64,128]{3,2,1,0:T(8,128)(2,1)S(1)}, u32[]{:S(2)}, u32[]{:S(2)}) async-start(bf16[16,8,64,128]{3,2,1,0:T(8,128)(2,1)} %bitcast.154), calls=%async_computation.2 | async-start | bytes 4194304 | tf_op jit(solution)/shard_map/all_to_all | solution.py:71
  62.5 6.0 copy-start.9
  62.5 162.2 %all-to-all-start.1 = ((bf16[16,8,64,576]{3,2,1,0:T(8,128)(2,1)}), bf16[16,8,64,576]{3,2,1,0:T(8,128)(2,1)}, u32[]{:S(2)}, u32[]{:S(2)}) async-start(bf16[16,8,64,576]{3,2,1,0:T(8,128)(2,1)} %bitcast.147), calls=%async_computation.1 | async-start | bytes 20971520 | tf_op jit(solution)/shard_map/all_to_all | solution.py:70
  67.8 532.1 %all-reduce.6.cloned.1.call-start = ((), (), s32[]{:S(2)}) async-start(), calls=%async_computation.5 | async-start | bytes 8388608 | tf_op jit(solution)/shard_map/psum | solution.py:111
  68.7 28.8 %copy-start.11 = (s32[128]{0:T(128)S(1)}, s32[128]{0:T(128)}, u32[]{:S(2)}) copy-start(s32[128]{0:T(128)} %param.18) | copy-start | bytes 1540
  68.7 28.9 %copy-start.12 = (f32[128,8]{0,1:T(8,128)S(1)}, f32[128,8]{0,1:T(8,128)}, u32[]{:S(2)}) copy-start(f32[128,8]{0,1:T(8,128)} %param.16) | copy-start | bytes 12292
  98.5 133.7 %copy-start.13 = (s32[64]{0:T(128)}, s32[64]{0:T(128)S(1)}, u32[]{:S(2)}) copy-start(s32[64]{0:T(128)S(1)} %fusion.44) | copy-start | bytes 772
  232.2 7.7 copy-start.6
  402.7 3.1 copy-start.5
  407.6 196.4 %copy-start.15 = (f32[128]{0:T(128)S(1)}, f32[128]{0:T(128)}, u32[]{:S(2)}) copy-start(f32[128]{0:T(128)} %param.19) | copy-start | bytes 1540
  599.9 4.1 copy-start.2
  599.9 4.1 copy-start.4
  606.2 3.0 copy-start.10
  657.5 2.5 copy-start.3
  657.5 2.5 copy-start.14
  669.1 5.9 copy-start.8
  669.1 61.5 %all-to-all-start.3 = ((f32[16,8,64,128]{3,2,1,0:T(8,128)}), f32[16,8,64,128]{3,2,1,0:T(8,128)}, u32[]{:S(2)}, u32[]{:S(2)}) async-start(f32[16,8,64,128]{3,2,1,0:T(8,128)} %bitcast.151), calls=%async_computation.3 | async-start | bytes 8388608 | tf_op jit(solution)/shard_map/all_to_all | solution.py:145
  674.4 271.9 %all-reduce.4.cloned.1.call-start = ((), (), s32[]{:S(2)}) async-start(), calls=%async_computation.4 | async-start | bytes 8388608 | tf_op jit(solution)/shard_map/psum | solution.py:151
  946.3 4.6 copy-start.1
Sparse Core Ops, SparseCore 0:
  407.7 192.1 all-reduce.5
  753.4 192.8 all-reduce.3
where the time goes:
time: 963 us; the launch traced here: 958 us
  waiting for transfers between devices  566 us (59%)
  other arithmetic  168 us (17%)
  local copies, waits for them, and re-layouts  126 us (13%)
  matrix products  56.5 us (6%)
  starting transfers between devices  14.7 us (2%)
  between operations  14.3 us (1%)
  blocking collectives  12.4 us (1%)
    psum x1, waiting for transfers between devices, shards(): key_grad = lax.psum(owned_grad.reshape(token_rows, index_width), 'head')  192 us
    psum x1, waiting for transfers between devices, shards(): summed_probs, index_scores = lax.psum((head_total, partial_scores), 'head')  192 us
    all_to_all x1, waiting for transfers between devices, shards(): lax.all_to_all(latent_blocks[asked_blocks], 'ctx', split_axis=0, concat_a...  123 us
    all_to_all x1, waiting for transfers between devices, shards(): lax.all_to_all(padded, 'ctx', split_axis=0, concat_axis=0, tiled=True)  54.9 us
    div x4, other arithmetic, masked_softmax(): return weights / jnp.sum(weights, axis=-1, keepdims=True)  50.9 us
    sub x4, other arithmetic, masked_softmax(): weights = jnp.where(visible, jnp.exp(values - highest), 0.0)  50.1 us
    dot_general x8, matrix products, row_product(): lax.dot_general(left, right, (((1,), (1,)), ((), ())), preferred_element_...  38 us
    gather x3, local copies, waits for them, and re-layouts, shards(): slot_of_query = position[selected]  23.2 us
  transfers between devices with their start and end apart: 5, of which 5 were waited for; matrix products, arithmetic and copies ran while one was open for 6% of the time, Pallas kernels for 0%

commit v1 on v0

v1 whole, which is shorter than its diff:
```python
import functools
import math

import jax
import jax.numpy as jnp
from jax import lax
from jax.experimental import pallas as pl
from jax.experimental.pallas import tpu as pltpu
from jax.sharding import PartitionSpec as P

HEADS = 128
BLK = 64
POOL = 64
NH = 8
NC = 16
LAT = 576
WIDTH = 128
QROWS = 16
SETB = POOL // NH
SETT = SETB * BLK
HALF = LAT // 2
SLOT = HALF + BLK
SETROWS = LAT * (SETT // 128) + SETT
UNION = POOL * BLK
IHEADS = 64

MESH = pl.DeviceIdType.MESH
ANY = pl.ANY
VM = pltpu.VMEM
DMA = pltpu.SemaphoreType.DMA

scale2 = 192.0 ** (-0.5) * math.log2(math.e)


def roll64(x):
    return pltpu.roll(x, 64, 1)


def start_barrier(me_h, me_c):
    barrier = pltpu.get_barrier_semaphore()
    for o in range(1, NH):
        pl.semaphore_signal(
            barrier, inc=1, device_id=(lax.rem(me_h + o, NH), me_c), device_id_type=MESH
        )
    for o in range(1, NC):
        pl.semaphore_signal(
            barrier, inc=1, device_id=(me_h, lax.rem(me_c + o, NC)), device_id_type=MESH
        )
    pl.semaphore_wait(barrier, NH + NC - 2)


def remote(src, dst, ssem, rsem, device):
    return pltpu.make_async_remote_copy(
        src_ref=src, dst_ref=dst, send_sem=ssem, recv_sem=rsem, device_id=device, device_id_type=MESH
    )


def gather_sets(own, out, half, me_h, me_c, ssem, rsem, lsem):
    right = (lax.rem(me_h + 2, NH), me_c)
    left = (lax.rem(me_h + 6, NH), me_c)
    flip = me_h + 1 - 2 * lax.rem(me_h, 2)
    partner = (flip, me_c)

    def flipped(h):
        return h + 1 - 2 * lax.rem(h, 2)

    started = []

    def go(src, dst, i, device):
        c = remote(src, dst, ssem.at[i], rsem.at[i], device)
        c.start()
        started.append(c)
        return c

    mine = pltpu.make_async_copy(own, out.at[me_h], lsem)
    mine.start()
    cy = go(own, out.at[me_h], 0, partner)
    cr = go(own, out.at[me_h], 1, right)
    cl = go(own, out.at[me_h], 2, left)
    remote(own, out.at[flip], ssem.at[0], rsem.at[0], partner).wait_recv()
    go(out.at[flip], out.at[flip], 3, right)
    go(out.at[flip], out.at[flip], 4, left)
    hl = lax.rem(me_h + 6, NH)
    hr = lax.rem(me_h + 2, NH)
    lo = pl.ds(0, half)
    hi = pl.ds(half, half)
    remote(own, out.at[hl], ssem.at[1], rsem.at[1], right).wait_recv()
    go(out.at[hl, lo], out.at[hl, lo], 5, right)
    remote(own, out.at[hr], ssem.at[2], rsem.at[2], left).wait_recv()
    go(out.at[hr, hi], out.at[hr, hi], 6, left)
    remote(own, out.at[flipped(hl)], ssem.at[3], rsem.at[3], right).wait_recv()
    go(out.at[flipped(hl), lo], out.at[flipped(hl), lo], 7, right)
    remote(own, out.at[flipped(hr)], ssem.at[4], rsem.at[4], left).wait_recv()
    go(out.at[flipped(hr), hi], out.at[flipped(hr), hi], 8, left)
    far = lax.rem(me_h + 4, NH)
    remote(out.at[far, lo], out.at[far, lo], ssem.at[5], rsem.at[5], right).wait_recv()
    remote(out.at[far, hi], out.at[far, hi], ssem.at[6], rsem.at[6], left).wait_recv()
    ff = flipped(far)
    remote(out.at[ff, lo], out.at[ff, lo], ssem.at[7], rsem.at[7], right).wait_recv()
    remote(out.at[ff, hi], out.at[ff, hi], ssem.at[8], rsem.at[8], left).wait_recv()
    mine.wait()
    for c in started:
        c.wait_send()


def iota(shape, dim):
    return lax.broadcasted_iota(jnp.int32, shape, dim)


def plan(sel, req_ref, tab_ref):
    hi = lax.shift_right_logical(sel, 7)
    lo = lax.bitwise_and(sel, 127)
    rows = sel.shape[0]
    owner_hot = jnp.concatenate(
        [jnp.where(iota((NC, 128), 0) == hi[i : i + 1, :], 1.0, 0.0) for i in range(rows)], axis=1
    ).astype(jnp.bfloat16)
    local_hot = jnp.concatenate(
        [jnp.where(iota((128, 128), 0) == lo[i : i + 1, :], 1.0, 0.0) for i in range(rows)], axis=1
    ).astype(jnp.bfloat16)
    counts = lax.dot_general(
        owner_hot, local_hot, (((1,), (1,)), ((), ())), preferred_element_type=jnp.float32
    )
    present = jnp.where(counts > 0.5, 1.0, 0.0)
    upper = jnp.where(iota((128, 128), 0) <= iota((128, 128), 1), 1.0, 0.0).astype(jnp.bfloat16)
    rank = jnp.dot(present.astype(jnp.bfloat16), upper, preferred_element_type=jnp.float32)
    total = rank[:, 127:128]
    lane = iota((NC, 128), 1)
    sub = iota((NC, 128), 0)
    spread = jnp.sum(jnp.where(lane == sub, total, 0.0), axis=0, keepdims=True)
    before = jnp.sum(jnp.where(lane < sub, jnp.broadcast_to(spread, (NC, 128)), 0.0), axis=1, keepdims=True)
    pos = (before + rank - 1.0).astype(jnp.int32)
    slot = lax.bitwise_and(pos, 7)
    step = lax.shift_right_logical(pos, 3).astype(jnp.float32)
    lane_f = lane.astype(jnp.float32)
    there = present > 0.5
    req = jnp.zeros((NC, 128), jnp.float32)
    ids = jnp.zeros((NC, 128), jnp.float32)
    owners = jnp.zeros((NC, 128), jnp.float32)
    sub_f = sub.astype(jnp.float32)
    for k in range(NH):
        hit = there & (slot == k)
        local = jnp.sum(jnp.where(hit, lane_f, 0.0), axis=1, keepdims=True)
        at = jnp.sum(jnp.where(hit, step, 0.0), axis=1, keepdims=True)
        has = jnp.sum(jnp.where(hit, 1.0, 0.0), axis=1, keepdims=True)
        req = jnp.where(lane == k, local, req)
        here = jnp.where(lane_f == at + float(SETB * k), has, 0.0)
        ids = ids + here * (sub_f * 128.0 + local)
        owners = owners + here * sub_f
        back = jnp.where(has > 0.5, at, float(SETB))
        row = jnp.sum(jnp.where(lane == sub, back, 0.0), axis=0, keepdims=True)
        tab_ref[8 + k : 9 + k, :] = row.astype(jnp.int32)
    tab_ref[0:1, :] = jnp.sum(ids, axis=0, keepdims=True).astype(jnp.int32)
    tab_ref[1:2, :] = jnp.sum(owners, axis=0, keepdims=True).astype(jnp.int32)
    tab_ref[2:8, :] = jnp.zeros((6, 128), jnp.int32)
    req_ref[...] = jnp.broadcast_to(req.astype(jnp.int32)[:, None, :], (NC, 8, 128))


def plan_kernel(sel_ref, req_ref, tab_ref):
    plan(sel_ref[...], req_ref, tab_ref)


def make_plan(sel_t):
    vm_spec = pl.BlockSpec(memory_space=VM)
    return pl.pallas_call(
        plan_kernel,
        name="plan",
        out_shape=(
            jax.ShapeDtypeStruct((NC, 8, 128), jnp.int32),
            jax.ShapeDtypeStruct((16, 128), jnp.int32),
        ),
        in_specs=[vm_spec],
        out_specs=(vm_spec, vm_spec),
        compiler_params=pltpu.CompilerParams(vmem_limit_bytes=32 << 20),
    )(sel_t)


def fetch_kernel(
    tab_s, req, lat_hbm, ik_hbm, mq_hbm, iq_hbm, w_hbm,
    set_out, mq_out, iq_out, w_out, asked_out,
    lat_v, ik_v, stage, recv, own, asked, asked_s,
    q_send, q_recv, i_send, i_recv, w_send, w_recv, r_send, r_recv, b_send, b_recv, g_send, g_recv, loc, l_sem,
):
    me_h = lax.axis_index("head")
    me_c = lax.axis_index("ctx")
    loads = [pltpu.make_async_copy(ik_hbm, ik_v, loc.at[1])] + [
        pltpu.make_async_copy(lat_hbm.at[:, pl.ds(i * 128, 128)], lat_v.at[i], l_sem.at[i])
        for i in range(lat_v.shape[0])
    ]
    for c in loads:
        c.start()
    my_q = pl.ds(pl.multiple_of(me_h * QROWS, QROWS), QROWS)
    own_copies = [
        pltpu.make_async_copy(mq_hbm.at[my_q], mq_out.at[me_h], loc.at[2]),
        pltpu.make_async_copy(iq_hbm.at[my_q], iq_out.at[me_h], loc.at[3]),
        pltpu.make_async_copy(w_hbm, w_out.at[me_h], loc.at[4]),
    ]
    for c in own_copies:
        c.start()
    start_barrier(me_h, me_c)
    sends = []
    own_req = pltpu.make_async_copy(req.at[me_c], asked.at[me_c], loc.at[6])
    own_req.start()
    for o in range(1, NC):
        c = lax.rem(me_c + o, NC)
        s = remote(req.at[c], asked.at[me_c], r_send.at[o], r_recv.at[o], (me_h, c))
        s.start()
        sends.append(s)
    for o in range(1, NH):
        h = lax.rem(me_h + o, NH)
        s = remote(
            mq_hbm.at[pl.ds(pl.multiple_of(h * QROWS, QROWS), QROWS)],
            mq_out.at[me_h], q_send.at[o], q_recv.at[o], (h, me_c),
        )
        s.start()
        sends.append(s)
        s = remote(
            iq_hbm.at[pl.ds(pl.multiple_of(h * QROWS, QROWS), QROWS)],
            iq_out.at[me_h], i_send.at[o], i_recv.at[o], (h, me_c),
        )
        s.start()
        sends.append(s)
        s = remote(w_hbm, w_out.at[me_h], w_send.at[o], w_recv.at[o], (h, me_c))
        s.start()
        sends.append(s)
    own_req.wait()
    for o in range(1, NC):
        c = lax.rem(me_c + NC - o, NC)
        remote(req.at[c], asked.at[c], r_send.at[o], r_recv.at[o], (me_h, c)).wait_recv()
    asked_out[...] = asked[:, 0, :]
    asked_copy = pltpu.make_async_copy(asked_out, asked_s, loc.at[7])
    asked_copy.start()
    for c in loads:
        c.wait()
    asked_copy.wait()
    first = iota((HALF, 128), 1) < 64
    for o in range(1, NC + 1):
        r = lax.rem(me_c + o, NC)
        b = asked_s[r, me_h]
        odd = jnp.full((HALF, 128), lax.bitwise_and(b, 1), jnp.int32) == 1
        pair = lax.shift_right_logical(b, 1)
        top = lat_v[pair, 0:HALF, :].astype(jnp.float32)
        bot = lat_v[pair, HALF:LAT, :].astype(jnp.float32)
        packed = jnp.where(
            first, jnp.where(odd, roll64(top), top), jnp.where(odd, bot, roll64(bot))
        ).astype(jnp.bfloat16)
        keys = ik_v[b]
        if o < NC:
            stage[o, 0:HALF, :] = packed
            stage[o, HALF:SLOT, :] = keys
            s = remote(stage.at[o], recv.at[me_c], b_send.at[o], b_recv.at[o], (me_h, r))
            s.start()
            sends.append(s)
        else:
            recv[me_c, 0:HALF, :] = packed
            recv[me_c, HALF:SLOT, :] = keys
    for o in range(1, NC):
        c = lax.rem(me_c + NC - o, NC)
        remote(stage.at[o], recv.at[c], b_send.at[o], b_recv.at[o], (me_h, c)).wait_recv()
    for i in range(SETB // 2):
        ca = tab_s[1, me_h * SETB + 2 * i]
        cb = tab_s[1, me_h * SETB + 2 * i + 1]
        a = recv[ca, 0:HALF, :].astype(jnp.float32)
        b = recv[cb, 0:HALF, :].astype(jnp.float32)
        own[i * LAT : i * LAT + HALF, :] = jnp.where(first, a, roll64(b)).astype(jnp.bfloat16)
        own[i * LAT + HALF : (i + 1) * LAT, :] = jnp.where(first, roll64(a), b).astype(jnp.bfloat16)
        base = LAT * (SETT // 128) + 2 * i * BLK
        own[base : base + BLK, :] = recv[ca, HALF:SLOT, :]
        own[base + BLK : base + 2 * BLK, :] = recv[cb, HALF:SLOT, :]
    gather_sets(own, set_out, SETROWS // 2, me_h, me_c, g_send, g_recv, loc.at[8])
    for o in range(1, NH):
        h = lax.rem(me_h + NH - o, NH)
        rows = pl.ds(0, QROWS)
        remote(mq_hbm.at[rows], mq_out.at[h], q_send.at[o], q_recv.at[o], (h, me_c)).wait_recv()
        remote(iq_hbm.at[rows], iq_out.at[h], i_send.at[o], i_recv.at[o], (h, me_c)).wait_recv()
        remote(w_hbm, w_out.at[h], w_send.at[o], w_recv.at[o], (h, me_c)).wait_recv()
    for c in own_copies:
        c.wait()
    for s in sends:
        s.wait_send()


def fetch(tab, req, lat_t, index_key, main_query, index_query, weight_t):
    any_spec = pl.BlockSpec(memory_space=ANY)
    vm_spec = pl.BlockSpec(memory_space=VM)
    bf, i32 = jnp.bfloat16, jnp.int32
    return pl.pallas_call(
        fetch_kernel,
        name="fetch",
        out_shape=(
            jax.ShapeDtypeStruct((NH, SETROWS, 128), bf),
            jax.ShapeDtypeStruct((NH, QROWS, main_query.shape[1]), bf),
            jax.ShapeDtypeStruct((NH, QROWS, index_query.shape[1]), bf),
            jax.ShapeDtypeStruct((NH, 8, 128), jnp.float32),
            jax.ShapeDtypeStruct((16, 128), i32),
        ),
        in_specs=[pl.BlockSpec(memory_space=pltpu.SMEM), vm_spec] + [any_spec] * 5,
        out_specs=(any_spec,) * 4 + (vm_spec,),
        scratch_shapes=[
            VM((lat_t.shape[1] // 128, LAT, 128), bf),
            VM(index_key.shape, bf),
            VM((NC, SLOT, 128), bf),
            VM((NC, SLOT, 128), bf),
            VM((SETROWS, 128), bf),
            VM((NC, 8, 128), i32),
            pltpu.SMEM((16, 128), i32),
            DMA((NH,)), DMA((NH,)), DMA((NH,)), DMA((NH,)), DMA((NH,)), DMA((NH,)),
            DMA((NC,)), DMA((NC,)), DMA((NC,)), DMA((NC,)),
            DMA((9,)), DMA((9,)), DMA((9,)), DMA((lat_t.shape[1] // 128,)),
        ],
        compiler_params=pltpu.CompilerParams(
            collective_id=0, has_side_effects=True, vmem_limit_bytes=32 << 20
        ),
    )(tab, req, lat_t, index_key, main_query, index_query, weight_t)


def core_kernel(
    tab_s, set_ref, mq_ref, iq_ref, w_ref, sel_ref, len_ref, cot_ref,
    ug_ref, iqg_ref, wg_ref,
    s_ref, pre_ref, edge_ref, bias_ref, tgt_ref, idx_ref, grad_ref, meta_ref, wq_ref, selb_ref, wb_ref, iqr_ref, qt_ref, ugt_ref, wcol_ref,
):
    me = lax.axis_index("head")
    mine = pl.ds(pl.multiple_of(me * QROWS, QROWS), QROWS)
    f32, bf = jnp.float32, jnp.bfloat16
    top = sel_ref.shape[0]
    meta_ref[...] = jnp.zeros((128, 128), f32)
    meta_ref[0:top, :] = sel_ref[...].astype(f32)
    meta_ref[top : top + 1, :] = len_ref[...].astype(f32)
    meta_ref[top + 1 : top + 2, :] = cot_ref[...]
    meta_ref[64 : 64 + IHEADS, :] = w_ref[...].reshape(IHEADS, 128)
    meta_ref[...] = meta_ref[...].T
    row = meta_ref[mine, :]
    for i in range(top):
        selb_ref[i] = jnp.broadcast_to(row[:, i : i + 1], (QROWS, 128))
    limit = jnp.broadcast_to(row[:, top : top + 1], (QROWS, 128))
    cot = row[:, top + 1 : top + 2]
    for j in range(IHEADS):
        wb_ref[j] = jnp.broadcast_to(row[:, 64 + j : 65 + j], (QROWS, 128))
    lane = iota((QROWS, 128), 1)

    def mask_tile(i, carry):
        b0 = tab_s[0, 2 * i]
        b1 = tab_s[0, 2 * i + 1]
        block = jnp.where(lane < 64, b0, b1)
        block_f = block.astype(f32)
        hit = selb_ref[0] == block_f
        for q in range(1, top):
            hit = hit | (selb_ref[q] == block_f)
        token = (block * BLK + lax.bitwise_and(lane, 63)).astype(f32)
        ok = hit & (token < limit)
        bias_ref[:, pl.ds(pl.multiple_of(i * 128, 128), 128)] = jnp.where(ok, 0.0, -jnp.inf)
        return carry

    lax.fori_loop(0, UNION // 128, mask_tile, 0)

    for h in range(NH):
        for k in range(8):
            iqr_ref[(h * 8 + k) * QROWS : (h * 8 + k + 1) * QROWS, :] = iq_ref[h, :, k * 128 : (k + 1) * 128]
    KEY0 = LAT * (SETT // 128)
    for h in range(NH):
        pre_ref[:, h * SETT : (h + 1) * SETT] = lax.dot_general(
            iqr_ref[...], set_ref[h, KEY0 : KEY0 + SETT, :], (((1,), (1,)), ((), ())), preferred_element_type=f32
        )
    CH = 512

    def index_chunk(i, carry):
        cols = pl.ds(pl.multiple_of(i * CH, CH), CH)
        acc = jnp.zeros((QROWS, CH), f32)
        for j in range(IHEADS):
            w = jnp.concatenate([wb_ref[j]] * (CH // 128), axis=1)
            acc = acc + w * jnp.maximum(pre_ref[j * QROWS : (j + 1) * QROWS, cols], 0.0)
        idx_ref[:, cols] = acc + bias_ref[:, cols]
        return carry

    lax.fori_loop(0, UNION // CH, index_chunk, 0)

    tgt_ref[...] = jnp.zeros((QROWS, UNION), f32)
    per = mq_ref.shape[2] // LAT

    def head_group(g, carry):
        for k in range(per):
            qt_ref[k * QROWS : (k + 1) * QROWS, :] = mq_ref[g, :, k * LAT : (k + 1) * LAT]
        for h in range(NH):
            for t in range(SETT // 256):
                keys = jnp.concatenate(
                    [set_ref[h, (2 * t + q) * LAT : (2 * t + q + 1) * LAT, :] for q in range(2)], axis=1
                )
                at = h * SETT + t * 256
                s_ref[:, at : at + 256] = jnp.dot(qt_ref[...], keys, preferred_element_type=f32)
        recips = []
        for k in range(per):
            rows = slice(k * QROWS, (k + 1) * QROWS)
            high = jnp.full((QROWS, 128), -jnp.inf, f32)
            for t in range(UNION // 128):
                cols = slice(t * 128, (t + 1) * 128)
                v = s_ref[rows, cols] + bias_ref[:, cols]
                s_ref[rows, cols] = v
                high = jnp.maximum(high, v)
            top_v = jnp.broadcast_to(jnp.max(high, axis=1, keepdims=True), (QROWS, 128))
            den = jnp.zeros((QROWS, 128), f32)
            for t in range(UNION // 128):
                cols = slice(t * 128, (t + 1) * 128)
                p = jnp.exp2((s_ref[rows, cols] - top_v) * scale2)
                s_ref[rows, cols] = p
                den = den + p
            recips.append(jnp.broadcast_to(1.0 / jnp.sum(den, axis=1, keepdims=True), (QROWS, 128)))
        for t in range(UNION // 128):
            cols = slice(t * 128, (t + 1) * 128)
            acc = tgt_ref[:, cols]
            for k in range(per):
                acc = acc + s_ref[k * QROWS : (k + 1) * QROWS, cols] * recips[k]
            tgt_ref[:, cols] = acc
        return carry

    lax.fori_loop(0, NH, head_group, 0)

    v = idx_ref[...]
    e = jnp.exp(v - jnp.max(v, axis=1, keepdims=True))
    chosen = e / jnp.sum(e, axis=1, keepdims=True)
    grad_ref[...] = cot * (chosen - tgt_ref[...] * (1.0 / HEADS))

    def back_head(j, carry):
        rows = pl.ds(pl.multiple_of(j * QROWS, QROWS), QROWS)
        w = wb_ref[j]
        total = jnp.zeros((QROWS, 128), f32)
        for t in range(UNION // 128):
            cols = slice(t * 128, (t + 1) * 128)
            pre = pre_ref[rows, cols]
            grad = grad_ref[:, cols]
            total = total + jnp.maximum(pre, 0.0) * grad
            edge_ref[rows, cols] = jnp.where(pre > 0.0, grad * w, 0.0).astype(bf)
        wcol_ref[j] = jnp.broadcast_to(jnp.sum(total, axis=1, keepdims=True), (QROWS, 128))
        return carry

    lax.fori_loop(0, IHEADS, back_head, 0)
    lane64 = iota((QROWS, 128), 1)
    wrow = jnp.zeros((QROWS, 128), f32)
    for j in range(IHEADS):
        wrow = jnp.where(lane64 == j, wcol_ref[j], wrow)
    wq_ref[...] = jnp.zeros((128, 128), f32)
    wq_ref[mine, :] = wrow
    wg_ref[...] = wq_ref[...].T[0:IHEADS, :].reshape(NH, 8, 128)

    iq_t = iqr_ref[...].T
    for h in range(NH):
        part = edge_ref[:, h * SETT : (h + 1) * SETT]
        ug_ref[h] = jnp.dot(iq_t, part, preferred_element_type=f32).T
    for g in range(NH):
        rows = slice(g * 128, (g + 1) * 128)
        acc = jnp.zeros((128, 128), f32)
        for h in range(NH):
            acc = acc + jnp.dot(
                edge_ref[rows, h * SETT : (h + 1) * SETT], set_ref[h, KEY0 : KEY0 + SETT, :], preferred_element_type=f32
            )
        for k in range(8):
            iqg_ref[g, :, k * 128 : (k + 1) * 128] = acc[k * QROWS : (k + 1) * QROWS, :]


def core(tab, sets, mq, iq, w, sel_t, lengths, cot):
    f32, bf = jnp.float32, jnp.bfloat16
    vm_spec = pl.BlockSpec(memory_space=VM)
    rows = IHEADS * QROWS
    return pl.pallas_call(
        core_kernel,
        name="core",
        out_shape=(
            jax.ShapeDtypeStruct((NH, SETT, 128), f32),
            jax.ShapeDtypeStruct((NH, QROWS, 1024), f32),
            jax.ShapeDtypeStruct((NH, 8, 128), f32),
        ),
        in_specs=[pl.BlockSpec(memory_space=pltpu.SMEM)] + [vm_spec] * 7,
        out_specs=(vm_spec,) * 3,
        scratch_shapes=[
            VM((256, UNION), f32),
            VM((rows, UNION), f32),
            VM((rows, UNION), bf),
            VM((QROWS, UNION), f32),
            VM((QROWS, UNION), f32),
            VM((QROWS, UNION), f32),
            VM((QROWS, UNION), f32),
            VM((128, 128), f32),
            VM((128, 128), f32),
            VM((32, QROWS, 128), f32),
            VM((IHEADS, QROWS, 128), f32),
            VM((rows, 128), bf),
            VM((256, LAT), bf),
            VM((128, SETT), f32),
            VM((IHEADS, QROWS, 128), f32),
        ],
        compiler_params=pltpu.CompilerParams(vmem_limit_bytes=58 << 20),
    )(tab, sets, mq, iq, w, sel_t, lengths, cot)


def return_kernel(
    tab_s, ug_hbm, iqg_hbm, wg_hbm,
    iqg_out, wg_out, kg_out,
    urecv, sums, slots, brecv, own, wrecv,
    u_send, u_recv, i_send, i_recv, w_send, w_recv, b_send, b_recv, g_send, g_recv, loc,
):
    me_h = lax.axis_index("head")
    me_c = lax.axis_index("ctx")
    own_copies = [
        pltpu.make_async_copy(ug_hbm.at[me_h], urecv.at[me_h], loc.at[0]),
        pltpu.make_async_copy(
            iqg_hbm.at[me_h], iqg_out.at[pl.ds(pl.multiple_of(me_h * QROWS, QROWS), QROWS)], loc.at[1]
        ),
        pltpu.make_async_copy(wg_hbm.at[me_h], wrecv.at[me_h], loc.at[2]),
    ]
    for c in own_copies:
        c.start()
    start_barrier(me_h, me_c)
    sends = []
    for o in range(1, NH):
        h = lax.rem(me_h + o, NH)
        s = remote(ug_hbm.at[h], urecv.at[me_h], u_send.at[o], u_recv.at[o], (h, me_c))
        s.start()
        sends.append(s)
    for o in range(1, NH):
        h = lax.rem(me_h + o, NH)
        s = remote(
            iqg_hbm.at[h], iqg_out.at[pl.ds(pl.multiple_of(me_h * QROWS, QROWS), QROWS)],
            i_send.at[o], i_recv.at[o], (h, me_c),
        )
        s.start()
        sends.append(s)
        s = remote(wg_hbm.at[h], wrecv.at[me_h], w_send.at[o], w_recv.at[o], (h, me_c))
        s.start()
        sends.append(s)
    own_copies[0].wait()
    for o in range(1, NH):
        h = lax.rem(me_h + NH - o, NH)
        remote(ug_hbm.at[h], urecv.at[h], u_send.at[o], u_recv.at[o], (h, me_c)).wait_recv()
    for j in range(SETB):
        acc = urecv[0, j * BLK : (j + 1) * BLK, :]
        for h in range(1, NH):
            acc = acc + urecv[h, j * BLK : (j + 1) * BLK, :]
        sums[j] = acc
    sums[SETB] = jnp.zeros((BLK, 128), jnp.float32)
    for o in range(1, NC + 1):
        c = lax.rem(me_c + o, NC)
        value = sums[tab_s[8 + me_h, c]]
        if o < NC:
            slots[o] = value
            s = remote(slots.at[o], brecv.at[me_c], b_send.at[o], b_recv.at[o], (me_h, c))
            s.start()
            sends.append(s)
        else:
            brecv[me_c] = value
    for o in range(1, NC):
        c = lax.rem(me_c + NC - o, NC)
        remote(slots.at[o], brecv.at[c], b_send.at[o], b_recv.at[o], (me_h, c)).wait_recv()
    for r in range(NC):
        own[r * BLK : (r + 1) * BLK, :] = brecv[r].astype(own.dtype)
    gather_sets(own, kg_out, NC * BLK // 2, me_h, me_c, g_send, g_recv, loc.at[3])
    for o in range(1, NH):
        h = lax.rem(me_h + NH - o, NH)
        remote(
            iqg_hbm.at[h], iqg_out.at[pl.ds(pl.multiple_of(h * QROWS, QROWS), QROWS)],
            i_send.at[o], i_recv.at[o], (h, me_c),
        ).wait_recv()
        remote(wg_hbm.at[h], wrecv.at[h], w_send.at[o], w_recv.at[o], (h, me_c)).wait_recv()
    own_copies[1].wait()
    own_copies[2].wait()
    acc = wrecv[0]
    for h in range(1, NH):
        acc = acc + wrecv[h]
    wg_out[...] = acc
    for s in sends:
        s.wait_send()


SENT = jnp.float32


def give_back(tab, ug, iqg, wg):
    f32 = jnp.float32
    any_spec = pl.BlockSpec(memory_space=ANY)
    return pl.pallas_call(
        return_kernel,
        name="give_back",
        out_shape=(
            jax.ShapeDtypeStruct((NH * QROWS, 1024), f32),
            jax.ShapeDtypeStruct((8, 128), f32),
            jax.ShapeDtypeStruct((NH, NC * BLK, 128), SENT),
        ),
        in_specs=[pl.BlockSpec(memory_space=pltpu.SMEM)] + [any_spec] * 3,
        out_specs=(any_spec, pl.BlockSpec(memory_space=VM), any_spec),
        scratch_shapes=[
            VM((NH, SETT, 128), f32),
            VM((SETB + 1, BLK, 128), f32),
            VM((NC, BLK, 128), f32),
            VM((NC, BLK, 128), f32),
            VM((NC * BLK, 128), SENT),
            VM((NH, 8, 128), f32),
            DMA((NH,)), DMA((NH,)), DMA((NH,)), DMA((NH,)), DMA((NH,)), DMA((NH,)),
            DMA((NC,)), DMA((NC,)),
            DMA((9,)), DMA((9,)), DMA((4,)),
        ],
        compiler_params=pltpu.CompilerParams(
            collective_id=1, has_side_effects=True, vmem_limit_bytes=32 << 20
        ),
    )(tab, ug, iqg, wg)


def scatter_kernel(asked_s, kg_ref, out_ref):
    out_ref[...] = jnp.zeros(out_ref.shape, jnp.float32)

    def one(i, carry):
        h = lax.shift_right_logical(i, 4)
        r = lax.bitwise_and(i, 15)
        b = asked_s[r, h]
        rows = pl.ds(pl.multiple_of(b * BLK, BLK), BLK)
        out_ref[rows, :] = out_ref[rows, :] + kg_ref[h, pl.ds(pl.multiple_of(r * BLK, BLK), BLK), :].astype(jnp.float32)
        return carry

    lax.fori_loop(0, NH * NC, one, 0)


def scatter(asked, kg, tokens):
    return pl.pallas_call(
        scatter_kernel,
        name="scatter",
        out_shape=jax.ShapeDtypeStruct((tokens, 128), jnp.float32),
        in_specs=[pl.BlockSpec(memory_space=pltpu.SMEM), pl.BlockSpec(memory_space=VM)],
        out_specs=pl.BlockSpec(memory_space=VM),
        compiler_params=pltpu.CompilerParams(vmem_limit_bytes=32 << 20),
    )(asked, kg)


def shards(main_query, latent, index_query, index_key, index_weight, selected, lengths, cotangent):
    sel_t = selected.T
    req, tab = make_plan(sel_t)
    sets, mq, iq, w, asked = fetch(
        tab, req, latent.T, index_key.reshape(-1, BLK, WIDTH), main_query, index_query, index_weight.T
    )
    ug, iqg, wg = core(tab, sets, mq, iq, w, sel_t, lengths[None, :], cotangent[None, :])
    query_grad, weight_grad, kg = give_back(tab, ug, iqg, wg)
    key_grad = scatter(asked, kg, latent.shape[0])
    return query_grad, weight_grad.T, key_grad


def solution(mesh):
    return jax.shard_map(
        shards,
        mesh=mesh,
        in_specs=(
            P("ctx", "head"),
            P("ctx", None),
            P("ctx", "head"),
            P("ctx", None),
            P("ctx", "head"),
            P("ctx", None),
            P("ctx"),
            P("ctx"),
        ),
        out_specs=(P("ctx", "head"), P("ctx", "head"), P("ctx", None)),
        check_vma=False,
    )
```

time: 963 us -> 272 us (0.28)
  waiting for transfers between devices: 566 us -> 0 us
  Pallas kernels: 0 us -> 248 us
  other arithmetic: 168 us -> 0 us
  local copies, waits for them, and re-layouts: 126 us -> 19.3 us
  matrix products: 56.5 us -> 0 us
  starting transfers between devices: 14.7 us -> 0 us
  between operations: 14.3 us -> 0.71 us
  blocking collectives: 12.4 us -> 0 us
    psum x2 -> x0, waiting for transfers between devices: 385 us -> none  [the longest x1 192 us: shards(): key_grad = lax.psum(owned_grad.reshape(token_rows, index_width), 'head')]
    pallas_call x0 -> x5, Pallas kernels: none -> 248 us  [the longest x1 112 us: fetch(): pl.pallas_call(fetch_kernel, name='fetch', out_shape=(jax.ShapeDtypeStruc...]
    all_to_all x3 -> x0, waiting for transfers between devices: 181 us -> none  [the longest x1 123 us: shards(): lax.all_to_all(latent_blocks[asked_blocks], 'ctx', split_axis=0, concat_a...]
    dot_general x16 -> x0, matrix products: 56.5 us -> none  [the longest x8 38 us: row_product(): lax.dot_general(left, right, (((1,), (1,)), ((), ())), preferred_element_...]
    div x4 -> x0, other arithmetic: 50.9 us -> none  [masked_softmax(): return weights / jnp.sum(weights, axis=-1, keepdims=True)]
    sub x5 -> x0, other arithmetic: 50.1 us -> none  [the longest x4 50.1 us: masked_softmax(): weights = jnp.where(visible, jnp.exp(values - highest), 0.0)]
    gather x8 -> x0, local copies, waits for them, and re-layouts: 46.1 us -> none  [the longest x3 23.2 us: shards(): slot_of_query = position[selected]]
    scatter-add x2 -> x0, other arithmetic: 29 us -> none  [the longest x1 20.1 us: shards(): owned_grad = jnp.zeros((blocks_each, BLK, index_width), jnp.float32).at[a...]
  transfers between devices with their start and end apart: 5 -> 0, of which waited for: 5 -> 0; matrix products, arithmetic and copies ran while one was open for 6% -> 0% of each run, Pallas kernels for 0% -> 0%
where the time goes in v1:
time: 272 us; the launch traced here: 268 us
  Pallas kernels  248 us (91%)
  local copies, waits for them, and re-layouts  19.3 us (7%)
    pallas_call x1, Pallas kernels, fetch(): pl.pallas_call(fetch_kernel, name='fetch', out_shape=(jax.ShapeDtypeStruc...  112 us
    pallas_call x1, Pallas kernels, give_back(): pl.pallas_call(return_kernel, name='give_back', out_shape=(jax.ShapeDtype...  85.1 us
    pallas_call x1, Pallas kernels, core(): pl.pallas_call(core_kernel, name='core', out_shape=(jax.ShapeDtypeStruct(...  45.6 us
    unnamed x32, local copies, waits for them, and re-layouts  19.3 us

profile of v1, /device:TPU:0, one launch (start us, length us, event | category | flops | bytes accessed | tf_op | source)
XLA Modules:
  0.0 268.1 jit_solution(14270637477642239476)
XLA Ops:
  0.6 0.0 copy-start.11
  0.6 0.7 copy-done.11
  1.4 0.8 plan.1
  2.2 0.0 copy-start.9
  2.2 0.0 copy-start
  2.2 3.7 %copy-done = bf16[8192,576]{0,1:T(8,128)(2,1)S(1)} copy-done((bf16[8192,576]{0,1:T(8,128)(2,1)S(1)}, bf16[8192,576]{0,1:T(8,128)(2,1)}, u32[]{:S(2)}) %copy-start) | copy-done | bytes 9437208
  5.9 0.0 copy-start.2
  5.9 1.7 copy-done.2
  7.5 0.0 copy-start.4
  7.5 1.6 copy-done.4
  9.1 0.0 copy-start.7
  9.1 0.9 copy-done.7
  10.1 0.0 copy-start.14
  10.1 0.7 copy-done.14
  10.8 112.3 %fetch.1 = (bf16[8,2816,128]{2,1,0:T(8,128)(2,1)S(1)}, bf16[8,16,9216]{2,1,0:T(8,128)(2,1)S(1)}, bf16[8,16,1024]{2,1,0:T(8,128)(2,1)S(1)}, f32[8,8,128]{2,1,0:T(8,128)S(1)}, s32[16,128]{1,0:T(8,128)S(1)}) custom-call(s32[16,128]{1,0:T(8,128)S(1)} %get-tuple-element.16.tab_s, s32[16,8,128]{2,1,0:T(8,128)S(1)} %get-tuple-element.17.req, ...), custom_call_target="tpu_custom_call" | custom-call | tf_op jit(solution)/shard_map/fetch/pallas_call | solution.py:286
  123.1 0.0 copy-done.9
  123.1 0.0 copy-start.1
  123.1 2.5 copy-done.1
  125.6 0.0 copy-start.3
  125.6 1.4 copy-done.3
  127.0 0.0 copy-start.8
  127.0 0.7 copy-done.8
  127.8 0.0 copy-start.12
  127.8 0.6 copy-done.12
  128.4 0.0 copy-start.10
  128.4 45.6 %core.1 = (f32[8,512,128]{2,1,0:T(8,128)}, f32[8,16,1024]{2,1,0:T(8,128)}, f32[8,8,128]{2,1,0:T(8,128)}) custom-call(s32[16,128]{1,0:T(8,128)} %copy-done.9, bf16[8,2816,128]{2,1,0:T(8,128)(2,1)} %copy-done.1, bf16[8,16,9216]{2,1,0:T(8,128)(2,1)} %copy-done.3, bf16[8,16,1024]{2,1,0:T(8,128)(2,1)} %copy-done.8, f32[8,8,128]{2,1,0:T(8,128)} %copy-done.12, ...), custom_call_target="tpu_custom_call" | custom-call | tf_op jit(solution)/shard_map/core/pallas_call | solution.py:462
  174.0 0.0 copy-done.10
  174.0 0.0 copy-start.5
  174.0 1.6 copy-done.5
  175.6 0.0 copy-start.6
  175.6 1.0 copy-done.6
  176.6 0.0 copy-start.13
  176.6 0.8 copy-done.13
  177.4 85.1 %give_back.1 = (f32[128,1024]{1,0:T(8,128)S(1)}, f32[8,128]{1,0:T(8,128)S(1)}, f32[8,1024,128]{2,1,0:T(8,128)S(1)}) custom-call(s32[16,128]{1,0:T(8,128)S(1)} %copy-done.10, f32[8,512,128]{2,1,0:T(8,128)S(1)} %copy-done.5, f32[8,16,1024]{2,1,0:T(8,128)S(1)} %copy-done.6, f32[8,8,128]{2,1,0:T(8,128)S(1)} %copy-done.13), custom_call_target="tpu_custom_call" | custom-call | tf_op jit(solution)/shard_map/give_back/pallas_call | solution.py:577
  262.5 4.3 %scatter.1 = f32[8192,128]{1,0:T(8,128)} custom-call(s32[16,128]{1,0:T(8,128)S(1)} %get-tuple-element.27.asked_s, f32[8,1024,128]{2,1,0:T(8,128)S(1)} %get-tuple-element.28.kg_ref), custom_call_target="tpu_custom_call" | custom-call | tf_op jit(solution)/shard_map/scatter/pallas_call | solution.py:619
  266.8 0.8 copy.13
  267.6 0.6 copy.14
Async XLA Ops:
  0.6 0.7 copy-start.11
  2.2 120.9 %copy-start.9 = (s32[16,128]{1,0:T(8,128)}, s32[16,128]{1,0:T(8,128)S(1)}, u32[]{:S(2)}) copy-start(s32[16,128]{1,0:T(8,128)S(1)} %get-tuple-element.16.tab_s) | copy-start | bytes 24580
  2.2 3.7 %copy-start = (bf16[8192,576]{0,1:T(8,128)(2,1)S(1)}, bf16[8192,576]{0,1:T(8,128)(2,1)}, u32[]{:S(2)}) copy-start(bf16[8192,576]{0,1:T(8,128)(2,1)} %param.9) | copy-start | bytes 28311556
  5.9 1.7 copy-start.2
  7.5 1.6 copy-start.4
  9.1 0.9 copy-start.7
  10.1 0.7 copy-start.14
  123.1 2.5 copy-start.1
  125.6 1.4 copy-start.3
  127.0 0.7 copy-start.8
  127.8 0.6 copy-start.12
  128.4 45.6 %copy-start.10 = (s32[16,128]{1,0:T(8,128)S(1)}, s32[16,128]{1,0:T(8,128)}, u32[]{:S(2)}) copy-start(s32[16,128]{1,0:T(8,128)} %copy-done.9) | copy-start | bytes 24580
  174.0 1.6 copy-start.5
  175.6 1.0 copy-start.6
  176.6 0.8 copy-start.13

commit v2 on v1

v2 whole, which is shorter than its diff:
```python
import functools
import math

import jax
import jax.numpy as jnp
from jax import lax
from jax.experimental import pallas as pl
from jax.experimental.pallas import tpu as pltpu
from jax.sharding import PartitionSpec as P

HEADS = 128
BLK = 64
POOL = 64
NH = 8
NC = 16
LAT = 576
WIDTH = 128
QROWS = 16
SETB = POOL // NH
SETT = SETB * BLK
HALF = LAT // 2
SLOT = HALF + BLK
UNION = POOL * BLK
IHEADS = 64

MESH = pl.DeviceIdType.MESH
ANY = pltpu.HBM
VM = pltpu.VMEM
DMA = pltpu.SemaphoreType.DMA

HIDDEN = -1e30
scale2 = 192.0 ** (-0.5) * math.log2(math.e)


def roll64(x):
    return pltpu.roll(x, 64, 1)


def start_barrier(me_h, me_c):
    barrier = pltpu.get_barrier_semaphore()
    for o in range(1, NH):
        pl.semaphore_signal(
            barrier, inc=1, device_id=(lax.rem(me_h + o, NH), me_c), device_id_type=MESH
        )
    for o in range(1, NC):
        pl.semaphore_signal(
            barrier, inc=1, device_id=(me_h, lax.rem(me_c + o, NC)), device_id_type=MESH
        )
    pl.semaphore_wait(barrier, NH + NC - 2)


def remote(src, dst, ssem, rsem, device):
    return pltpu.make_async_remote_copy(
        src_ref=src, dst_ref=dst, send_sem=ssem, recv_sem=rsem, device_id=device, device_id_type=MESH
    )


def gather_sets(pieces, me_h, me_c, ssem, rsem, lsem, between=None):
    right = (lax.rem(me_h + 2, NH), me_c)
    left = (lax.rem(me_h + 6, NH), me_c)
    flip = me_h + 1 - 2 * lax.rem(me_h, 2)
    partner = (flip, me_c)
    hl = lax.rem(me_h + 6, NH)
    hr = lax.rem(me_h + 2, NH)
    far = lax.rem(me_h + 4, NH)

    def flipped(h):
        return h + 1 - 2 * lax.rem(h, 2)

    count = len(pieces)
    sent = []

    def part(n, which):
        own, out, start, rows = pieces[n]
        half = rows // 32 * 16
        if which == 0:
            return start, rows
        return (start, half) if which == 1 else (start + half, rows - half)

    def copy(n, i, h, which, device, first=False):
        own, out, _, _ = pieces[n]
        start, rows = part(n, which)
        dst = out.at[h, pl.ds(start, rows)]
        src = own.at[pl.ds(start, rows)] if first else dst
        return remote(src, dst, ssem.at[i * count + n], rsem.at[i * count + n], device)

    def go(i, h, which, device, first=False):
        for n in range(count):
            c = copy(n, i, h, which, device, first)
            c.start()
            sent.append(c)

    def wait(i, h, which, device):
        for n in range(count):
            copy(n, i, h, which, device).wait_recv()

    locals_ = [
        pltpu.make_async_copy(own.at[pl.ds(start, rows)], out.at[me_h, pl.ds(start, rows)], lsem.at[n])
        for n, (own, out, start, rows) in enumerate(pieces)
    ]
    for c in locals_:
        c.start()
    go(0, me_h, 0, partner, True)
    go(1, me_h, 0, right, True)
    go(2, me_h, 0, left, True)
    yield
    wait(0, flip, 0, partner)
    go(3, flip, 0, right)
    go(4, flip, 0, left)
    yield
    wait(1, hl, 0, right)
    go(5, hl, 1, right)
    wait(2, hr, 0, left)
    go(6, hr, 2, left)
    yield
    wait(3, flipped(hl), 0, right)
    go(7, flipped(hl), 1, right)
    wait(4, flipped(hr), 0, left)
    go(8, flipped(hr), 2, left)
    yield
    wait(5, far, 1, right)
    wait(6, far, 2, left)
    wait(7, flipped(far), 1, right)
    wait(8, flipped(far), 2, left)
    for c in locals_:
        c.wait()
    for c in sent:
        c.wait_send()


def finish(*stages):
    left = list(stages)
    while left:
        for g in list(left):
            if next(g, 0) == 0:
                left.remove(g)


def iota(shape, dim):
    return lax.broadcasted_iota(jnp.int32, shape, dim)


def plan(sel, req_ref, tab_ref):
    hi = lax.shift_right_logical(sel, 7)
    lo = lax.bitwise_and(sel, 127)
    rows = sel.shape[0]
    owner_hot = jnp.concatenate(
        [jnp.where(iota((NC, 128), 0) == hi[i : i + 1, :], 1.0, 0.0) for i in range(rows)], axis=1
    ).astype(jnp.bfloat16)
    local_hot = jnp.concatenate(
        [jnp.where(iota((128, 128), 0) == lo[i : i + 1, :], 1.0, 0.0) for i in range(rows)], axis=1
    ).astype(jnp.bfloat16)
    counts = lax.dot_general(
        owner_hot, local_hot, (((1,), (1,)), ((), ())), preferred_element_type=jnp.float32
    )
    present = jnp.where(counts > 0.5, 1.0, 0.0)
    upper = jnp.where(iota((128, 128), 0) <= iota((128, 128), 1), 1.0, 0.0).astype(jnp.bfloat16)
    rank = jnp.dot(present.astype(jnp.bfloat16), upper, preferred_element_type=jnp.float32)
    total = rank[:, 127:128]
    lane = iota((NC, 128), 1)
    sub = iota((NC, 128), 0)
    spread = jnp.sum(jnp.where(lane == sub, total, 0.0), axis=0, keepdims=True)
    before = jnp.sum(jnp.where(lane < sub, jnp.broadcast_to(spread, (NC, 128)), 0.0), axis=1, keepdims=True)
    pos = (before + rank - 1.0).astype(jnp.int32)
    slot = lax.bitwise_and(pos, 7)
    step = lax.shift_right_logical(pos, 3).astype(jnp.float32)
    lane_f = lane.astype(jnp.float32)
    there = present > 0.5
    req = jnp.zeros((NC, 128), jnp.float32)
    ids = jnp.zeros((NC, 128), jnp.float32)
    owners = jnp.zeros((NC, 128), jnp.float32)
    sub_f = sub.astype(jnp.float32)
    for k in range(NH):
        hit = there & (slot == k)
        local = jnp.sum(jnp.where(hit, lane_f, 0.0), axis=1, keepdims=True)
        at = jnp.sum(jnp.where(hit, step, 0.0), axis=1, keepdims=True)
        has = jnp.sum(jnp.where(hit, 1.0, 0.0), axis=1, keepdims=True)
        req = jnp.where(lane == k, local, req)
        here = jnp.where(lane_f == at + float(SETB * k), has, 0.0)
        ids = ids + here * (sub_f * 128.0 + local)
        owners = owners + here * sub_f
        back = jnp.where(has > 0.5, at, float(SETB))
        row = jnp.sum(jnp.where(lane == sub, back, 0.0), axis=0, keepdims=True)
        tab_ref[8 + k : 9 + k, :] = row.astype(jnp.int32)
    tab_ref[0:1, :] = jnp.sum(ids, axis=0, keepdims=True).astype(jnp.int32)
    tab_ref[1:2, :] = jnp.sum(owners, axis=0, keepdims=True).astype(jnp.int32)
    tab_ref[2:8, :] = jnp.zeros((6, 128), jnp.int32)
    req_ref[...] = jnp.broadcast_to(req.astype(jnp.int32)[:, None, :], (NC, 8, 128))


def plan_kernel(sel_ref, req_ref, tab_ref):
    plan(sel_ref[...], req_ref, tab_ref)


def make_plan(sel_t):
    vm_spec = pl.BlockSpec(memory_space=VM)
    return pl.pallas_call(
        plan_kernel,
        name="plan",
        out_shape=(
            jax.ShapeDtypeStruct((NC, 8, 128), jnp.int32),
            jax.ShapeDtypeStruct((16, 128), jnp.int32),
        ),
        in_specs=[vm_spec],
        out_specs=(vm_spec, vm_spec),
        compiler_params=pltpu.CompilerParams(vmem_limit_bytes=60 << 20),
    )(sel_t)


SPLIT = HALF // 2


def fetch_kernel(
    tab_s, req, lat_hbm, ik_hbm, mq_hbm, iq_hbm, w_hbm,
    kt_out, ik_out, mq_out, iq_out, w_out, asked_out,
    lat_v, ik_v, stage, recv_a, recv_b, own, own_ik, asked, asked_s,
    q_send, q_recv, i_send, i_recv, w_send, w_recv, r_send, r_recv, b_send, b_recv, c_send, c_recv,
    g_send, g_recv, h_send, h_recv, loc, loc_a, loc_b, l_sem,
):
    me_h = lax.axis_index("head")
    me_c = lax.axis_index("ctx")
    loads = [pltpu.make_async_copy(ik_hbm, ik_v, loc.at[1])] + [
        pltpu.make_async_copy(lat_hbm.at[:, pl.ds(i * 128, 128)], lat_v.at[i], l_sem.at[i])
        for i in range(lat_v.shape[0])
    ]
    for c in loads:
        c.start()
    my_q = pl.ds(pl.multiple_of(me_h * QROWS, QROWS), QROWS)
    own_copies = [
        pltpu.make_async_copy(mq_hbm.at[my_q], mq_out.at[me_h], loc.at[2]),
        pltpu.make_async_copy(iq_hbm.at[my_q], iq_out.at[me_h], loc.at[3]),
        pltpu.make_async_copy(w_hbm, w_out.at[me_h], loc.at[4]),
    ]
    for c in own_copies:
        c.start()
    start_barrier(me_h, me_c)
    sends = []
    own_req = pltpu.make_async_copy(req.at[me_c], asked.at[me_c], loc.at[6])
    own_req.start()
    for o in range(1, NC):
        c = lax.rem(me_c + o, NC)
        s = remote(req.at[c], asked.at[me_c], r_send.at[o], r_recv.at[o], (me_h, c))
        s.start()
        sends.append(s)

    def send_queries(o):
        h = lax.rem(me_h + o, NH)
        rows = pl.ds(pl.multiple_of(h * QROWS, QROWS), QROWS)
        for src, dst, ss, rs in (
            (mq_hbm.at[rows], mq_out, q_send, q_recv),
            (iq_hbm.at[rows], iq_out, i_send, i_recv),
            (w_hbm, w_out, w_send, w_recv),
        ):
            s = remote(src, dst.at[me_h], ss.at[o], rs.at[o], (h, me_c))
            s.start()
            sends.append(s)

    for o in (2, 6, 4):
        send_queries(o)
    own_req.wait()
    for o in range(1, NC):
        c = lax.rem(me_c + NC - o, NC)
        remote(req.at[c], asked.at[c], r_send.at[o], r_recv.at[o], (me_h, c)).wait_recv()
    asked_out[...] = asked[:, 0, :]
    asked_copy = pltpu.make_async_copy(asked_out, asked_s, loc.at[7])
    asked_copy.start()
    for c in loads:
        c.wait()
    asked_copy.wait()
    first = iota((HALF, 128), 1) < 64
    lower = pl.ds(0, SPLIT)
    upper = pl.ds(SPLIT, SLOT - SPLIT)
    late = []
    for o in range(1, NC + 1):
        r = lax.rem(me_c + o, NC)
        b = asked_s[r, me_h]
        odd = jnp.full((HALF, 128), lax.bitwise_and(b, 1), jnp.int32) == 1
        pair = lax.shift_right_logical(b, 1)
        top = lat_v[pair, 0:HALF, :].astype(jnp.float32)
        bot = lat_v[pair, HALF:LAT, :].astype(jnp.float32)
        packed = jnp.where(
            first, jnp.where(odd, roll64(top), top), jnp.where(odd, bot, roll64(bot))
        ).astype(jnp.bfloat16)
        keys = ik_v[b]
        if o < NC:
            stage[o, 0:HALF, :] = packed
            stage[o, HALF:SLOT, :] = keys
            s = remote(stage.at[o, lower], recv_a.at[me_c], b_send.at[o], b_recv.at[o], (me_h, r))
            s.start()
            sends.append(s)
            late.append(remote(stage.at[o, upper], recv_b.at[me_c], c_send.at[o], c_recv.at[o], (me_h, r)))
        else:
            recv_a[me_c] = packed[0:SPLIT]
            recv_b[me_c, 0 : HALF - SPLIT, :] = packed[SPLIT:HALF]
            recv_b[me_c, HALF - SPLIT : SLOT - SPLIT, :] = keys
    for s in late:
        s.start()
        sends.append(s)
    owners = [tab_s[1, me_h * SETB + j] for j in range(SETB)]

    def merge(lo, hi, recv):
        here = iota((hi - lo, 128), 1) < 64
        for i in range(SETB // 2):
            cols = slice(i * 128, (i + 1) * 128)
            a = recv[owners[2 * i], 0 : hi - lo, :].astype(jnp.float32)
            b = recv[owners[2 * i + 1], 0 : hi - lo, :].astype(jnp.float32)
            own[lo:hi, cols] = jnp.where(here, a, roll64(b)).astype(jnp.bfloat16)
            own[HALF + lo : HALF + hi, cols] = jnp.where(here, roll64(a), b).astype(jnp.bfloat16)

    for o in range(1, NC):
        c = lax.rem(me_c + NC - o, NC)
        remote(stage.at[o, lower], recv_a.at[c], b_send.at[o], b_recv.at[o], (me_h, c)).wait_recv()
    merge(0, SPLIT, recv_a)
    ga = gather_sets(
        [(own, kt_out, 0, SPLIT), (own, kt_out, HALF, SPLIT)], me_h, me_c, g_send, g_recv, loc_a
    )
    next(ga)
    for o in range(1, NC):
        c = lax.rem(me_c + NC - o, NC)
        remote(stage.at[o, upper], recv_b.at[c], c_send.at[o], c_recv.at[o], (me_h, c)).wait_recv()
    merge(SPLIT, HALF, recv_b)
    for j in range(SETB):
        own_ik[j * BLK : (j + 1) * BLK, :] = recv_b[owners[j], HALF - SPLIT : SLOT - SPLIT, :]
    gb = gather_sets(
        [(own, kt_out, SPLIT, HALF - SPLIT), (own, kt_out, HALF + SPLIT, HALF - SPLIT), (own_ik, ik_out, 0, SETT)],
        me_h, me_c, h_send, h_recv, loc_b,
    )
    next(gb)
    for o in (1, 7, 3, 5):
        send_queries(o)
    finish(ga, gb)
    for o in range(1, NH):
        h = lax.rem(me_h + NH - o, NH)
        rows = pl.ds(0, QROWS)
        remote(mq_hbm.at[rows], mq_out.at[h], q_send.at[o], q_recv.at[o], (h, me_c)).wait_recv()
        remote(iq_hbm.at[rows], iq_out.at[h], i_send.at[o], i_recv.at[o], (h, me_c)).wait_recv()
        remote(w_hbm, w_out.at[h], w_send.at[o], w_recv.at[o], (h, me_c)).wait_recv()
    for c in own_copies:
        c.wait()
    for s in sends:
        s.wait_send()


def fetch(tab, req, lat_t, index_key, main_query, index_query, weight_t):
    any_spec = pl.BlockSpec(memory_space=ANY)
    vm_spec = pl.BlockSpec(memory_space=VM)
    bf, i32 = jnp.bfloat16, jnp.int32
    return pl.pallas_call(
        fetch_kernel,
        name="fetch",
        out_shape=(
            jax.ShapeDtypeStruct((NH, LAT, SETT), bf),
            jax.ShapeDtypeStruct((NH, SETT, 128), bf),
            jax.ShapeDtypeStruct((NH, QROWS, main_query.shape[1]), bf),
            jax.ShapeDtypeStruct((NH, QROWS, index_query.shape[1]), bf),
            jax.ShapeDtypeStruct((NH, 8, 128), jnp.float32),
            jax.ShapeDtypeStruct((16, 128), i32),
        ),
        in_specs=[pl.BlockSpec(memory_space=pltpu.SMEM), vm_spec] + [any_spec] * 5,
        out_specs=(any_spec,) * 5 + (vm_spec,),
        scratch_shapes=[
            VM((lat_t.shape[1] // 128, LAT, 128), bf),
            VM(index_key.shape, bf),
            VM((NC, SLOT, 128), bf),
            VM((NC, SPLIT, 128), bf),
            VM((NC, SLOT - SPLIT, 128), bf),
            VM((LAT, SETT), bf),
            VM((SETT, 128), bf),
            VM((NC, 8, 128), i32),
            pltpu.SMEM((16, 128), i32),
            DMA((NH,)), DMA((NH,)), DMA((NH,)), DMA((NH,)), DMA((NH,)), DMA((NH,)),
            DMA((NC,)), DMA((NC,)), DMA((NC,)), DMA((NC,)), DMA((NC,)), DMA((NC,)),
            DMA((18,)), DMA((18,)), DMA((27,)), DMA((27,)), DMA((9,)), DMA((3,)), DMA((3,)),
            DMA((lat_t.shape[1] // 128,)),
        ],
        compiler_params=pltpu.CompilerParams(
            collective_id=0, has_side_effects=True, vmem_limit_bytes=60 << 20
        ),
    )(tab, req, lat_t, index_key, main_query, index_query, weight_t)


AUG = LAT + QROWS
TILE = 256


def core_kernel(
    tab_s, kt_hbm, ik_hbm, mq_ref, iq_ref, w_ref, sel_ref, len_ref, cot_ref,
    ug_ref, iqg_ref, wg_ref,
    kt_ref, ik_ref, sa_ref, sb_ref, ma_ref, mb_ref, qt_ref, pre_ref, ea_ref, eb_ref, bias_ref, tgt_ref, idx_ref,
    grad_ref, meta_ref, wq_ref, selb_ref, wb_ref, iqr_ref, wcol_ref, iqg_acc, sem_k, sem_i,
):
    me = lax.axis_index("head")
    mine = pl.ds(pl.multiple_of(me * QROWS, QROWS), QROWS)
    f32, bf = jnp.float32, jnp.bfloat16
    i_loads, k_loads = [], []
    for h in range(NH):
        i_loads.append(pltpu.make_async_copy(ik_hbm.at[h], ik_ref.at[pl.ds(h * SETT, SETT)], sem_i.at[h]))
        k_loads.append(
            pltpu.make_async_copy(
                kt_hbm.at[h], kt_ref.at[pl.ds(0, LAT), pl.ds(h * SETT, SETT)], sem_k.at[h]
            )
        )
    for c in i_loads + k_loads:
        c.start()
    top = sel_ref.shape[0]
    meta_ref[...] = jnp.zeros((128, 128), f32)
    meta_ref[0:top, :] = sel_ref[...].astype(f32)
    meta_ref[top : top + 1, :] = len_ref[...].astype(f32)
    meta_ref[top + 1 : top + 2, :] = cot_ref[...]
    meta_ref[64 : 64 + IHEADS, :] = w_ref[...].reshape(IHEADS, 128)
    meta_ref[...] = meta_ref[...].T
    row = meta_ref[mine, :]
    for i in range(top):
        selb_ref[i] = jnp.broadcast_to(row[:, i : i + 1], (QROWS, 128))
    limit = jnp.broadcast_to(row[:, top : top + 1], (QROWS, 128))
    cot = row[:, top + 1 : top + 2]
    for j in range(IHEADS):
        wb_ref[j] = jnp.broadcast_to(row[:, 64 + j : 65 + j], (QROWS, 128))
    lane = iota((QROWS, 128), 1)

    def mask_tile(i, carry):
        block = jnp.where(lane < 64, tab_s[0, 2 * i], tab_s[0, 2 * i + 1])
        block_f = block.astype(f32)
        hit = selb_ref[0] == block_f
        for q in range(1, top):
            hit = hit | (selb_ref[q] == block_f)
        token = (block * BLK + lax.bitwise_and(lane, 63)).astype(f32)
        ok = hit & (token < limit)
        cols = pl.ds(pl.multiple_of(i * 128, 128), 128)
        off = jnp.where(ok, 0.0, HIDDEN)
        bias_ref[:, cols] = off
        kt_ref[LAT:AUG, cols] = off.astype(bf)
        return carry

    lax.fori_loop(0, UNION // 128, mask_tile, 0)

    for h in range(NH):
        for k in range(8):
            iqr_ref[(h * 8 + k) * QROWS : (h * 8 + k + 1) * QROWS, :] = iq_ref[h, :, k * 128 : (k + 1) * 128]
    for c in i_loads:
        c.wait()

    def index_chunk(i, carry):
        cols = pl.ds(pl.multiple_of(i * SETT, SETT), SETT)
        acc = jnp.zeros((QROWS, SETT), f32)
        for b in range(4):
            rows = slice(b * 256, (b + 1) * 256)
            pre = lax.dot_general(
                iqr_ref[rows, :], ik_ref[cols, :], (((1,), (1,)), ((), ())), preferred_element_type=f32
            )
            pre_ref[rows, cols] = pre
            for j in range(16):
                w = jnp.concatenate([wb_ref[b * 16 + j]] * (SETT // 128), axis=1)
                acc = acc + w * jnp.maximum(pre[j * QROWS : (j + 1) * QROWS, :], 0.0)
        idx_ref[:, cols] = acc + bias_ref[:, cols]
        return carry

    lax.fori_loop(0, NH, index_chunk, 0)

    tgt_ref[...] = jnp.zeros((QROWS, UNION), f32)
    per = mq_ref.shape[2] // LAT
    hot = jnp.where(iota((QROWS, QROWS), 0) == iota((QROWS, QROWS), 1), 1.0, 0.0).astype(bf)
    for k in range(per):
        qt_ref[k * QROWS : (k + 1) * QROWS, LAT:AUG] = hot
    for c in k_loads:
        c.wait()

    def load_queries(g):
        for k in range(per):
            qt_ref[k * QROWS : (k + 1) * QROWS, 0:LAT] = mq_ref[g, :, k * LAT : (k + 1) * LAT]

    def score_tile(t, s_ref, m_ref):
        cols = slice(t * TILE, (t + 1) * TILE)
        s = jnp.dot(qt_ref[...], kt_ref[:, cols], preferred_element_type=f32)
        s_ref[:, cols] = s
        m = jnp.maximum(s[:, 0:128], s[:, 128:256])
        m_ref[...] = m if t == 0 else jnp.maximum(m_ref[...], m)

    def soften(k, s_ref, m_ref):
        rows = slice(k * QROWS, (k + 1) * QROWS)
        high = jnp.max(m_ref[rows, :], axis=1, keepdims=True) * scale2
        high = jnp.broadcast_to(high, (QROWS, 128))
        den = jnp.zeros((QROWS, 128), f32)
        for t in range(UNION // 128):
            cols = slice(t * 128, (t + 1) * 128)
            p = jnp.exp2(s_ref[rows, cols] * scale2 - high)
            s_ref[rows, cols] = p
            den = den + p
        return jnp.broadcast_to(1.0 / jnp.sum(den, axis=1, keepdims=True), (QROWS, 128))

    def add_up(recips, s_ref, lo):
        for t in range(UNION // 128):
            cols = slice(t * 128, (t + 1) * 128)
            acc = tgt_ref[:, cols]
            for q, r in enumerate(recips):
                acc = acc + s_ref[(lo + q) * QROWS : (lo + q + 1) * QROWS, cols] * r
            tgt_ref[:, cols] = acc

    def both(s_ref, m_ref, next_s, next_m):
        recips = []
        for k in range(per):
            recips.append(soften(k, s_ref, m_ref))
            if next_s is not None:
                score_tile(k, next_s, next_m)
            if k % 8 == 7:
                add_up(recips, s_ref, k - 7)
                recips = []

    load_queries(0)
    for t in range(UNION // TILE):
        score_tile(t, sa_ref, ma_ref)

    def two_groups(i, carry):
        load_queries(2 * i + 1)
        both(sa_ref, ma_ref, sb_ref, mb_ref)
        load_queries(2 * i + 2)
        both(sb_ref, mb_ref, sa_ref, ma_ref)
        return carry

    lax.fori_loop(0, NH // 2 - 1, two_groups, 0)
    load_queries(NH - 1)
    both(sa_ref, ma_ref, sb_ref, mb_ref)
    both(sb_ref, mb_ref, None, None)

    v = idx_ref[...]
    e = jnp.exp(v - jnp.max(v, axis=1, keepdims=True))
    chosen = e / jnp.sum(e, axis=1, keepdims=True)
    grad_ref[...] = cot * (chosen - tgt_ref[...] * (1.0 / HEADS))

    wcol_ref[...] = jnp.zeros(wcol_ref.shape, f32)
    iqg_acc[...] = jnp.zeros(iqg_acc.shape, f32)
    iq_t = iqr_ref[...].T

    def edges(h, e_ref):
        cols = pl.ds(pl.multiple_of(h * SETT, SETT), SETT)
        grad = grad_ref[:, cols]
        for j in range(IHEADS):
            rows = slice(j * QROWS, (j + 1) * QROWS)
            pre = pre_ref[rows, cols]
            w = jnp.concatenate([wb_ref[j]] * (SETT // 128), axis=1)
            part = jnp.maximum(pre, 0.0) * grad
            wcol_ref[j] = wcol_ref[j] + sum(part[:, t * 128 : (t + 1) * 128] for t in range(SETT // 128))
            e_ref[rows, :] = jnp.where(pre > 0.0, grad * w, 0.0).astype(bf)

    def products(h, e_ref):
        part = jnp.dot(iq_t, e_ref[...], preferred_element_type=f32).T.reshape(SETB, 2, BLK // 2, 128)
        for q in range(2):
            ug_ref[q, h] = part[:, q].reshape(SETT // 2, 128)
        keys = ik_ref[pl.ds(pl.multiple_of(h * SETT, SETT), SETT), :]
        for b in range(4):
            rows = slice(b * 256, (b + 1) * 256)
            iqg_acc[rows, :] = iqg_acc[rows, :] + jnp.dot(e_ref[rows, :], keys, preferred_element_type=f32)

    edges(0, ea_ref)

    def two_sets(i, carry):
        edges(2 * i + 1, eb_ref)
        products(2 * i, ea_ref)
        edges(2 * i + 2, ea_ref)
        products(2 * i + 1, eb_ref)
        return carry

    lax.fori_loop(0, NH // 2 - 1, two_sets, 0)
    edges(NH - 1, eb_ref)
    products(NH - 2, ea_ref)
    products(NH - 1, eb_ref)
    wrow = jnp.zeros((QROWS, 128), f32)
    for j in range(IHEADS):
        wrow = jnp.where(lane == j, jnp.sum(wcol_ref[j], axis=1, keepdims=True), wrow)
    wq_ref[...] = jnp.zeros((128, 128), f32)
    wq_ref[mine, :] = wrow
    wg_ref[...] = wq_ref[...].T[0:IHEADS, :].reshape(NH, 8, 128)
    for g in range(NH):
        for k in range(8):
            j = g * 8 + k
            iqg_ref[g, :, k * 128 : (k + 1) * 128] = iqg_acc[j * QROWS : (j + 1) * QROWS, :]


def core(tab, kt, ik, mq, iq, w, sel_t, lengths, cot):
    f32, bf = jnp.float32, jnp.bfloat16
    vm_spec = pl.BlockSpec(memory_space=VM)
    rows = IHEADS * QROWS
    return pl.pallas_call(
        core_kernel,
        name="core",
        out_shape=(
            jax.ShapeDtypeStruct((2, NH, SETT // 2, 128), f32),
            jax.ShapeDtypeStruct((NH, QROWS, 1024), f32),
            jax.ShapeDtypeStruct((NH, 8, 128), f32),
        ),
        in_specs=[pl.BlockSpec(memory_space=pltpu.SMEM), pl.BlockSpec(memory_space=ANY), pl.BlockSpec(memory_space=ANY)]
        + [vm_spec] * 6,
        out_specs=(vm_spec,) * 3,
        scratch_shapes=[
            VM((AUG, UNION), bf),
            VM((UNION, 128), bf),
            VM((256, UNION), f32),
            VM((256, UNION), f32),
            VM((256, 128), f32),
            VM((256, 128), f32),
            VM((256, AUG), bf),
            VM((rows, UNION), f32),
            VM((rows, SETT), bf),
            VM((rows, SETT), bf),
            VM((QROWS, UNION), f32),
            VM((QROWS, UNION), f32),
            VM((QROWS, UNION), f32),
            VM((QROWS, UNION), f32),
            VM((128, 128), f32),
            VM((128, 128), f32),
            VM((32, QROWS, 128), f32),
            VM((IHEADS, QROWS, 128), f32),
            VM((rows, 128), bf),
            VM((IHEADS, QROWS, 128), f32),
            VM((rows, 128), f32),
            DMA((NH,)),
            DMA((NH,)),
        ],
        compiler_params=pltpu.CompilerParams(vmem_limit_bytes=60 << 20),
    )(tab, kt, ik, mq, iq, w, sel_t, lengths, cot)


HB = BLK // 2


def return_kernel(
    tab_s, ug_hbm, iqg_hbm, wg_hbm,
    iqg_out, wg_out, kg_out,
    urecv, sums, slots, brecv, own, wrecv,
    u_send, u_recv, i_send, i_recv, w_send, w_recv, b_send, b_recv, g_send, g_recv, h_send, h_recv, loc, loc_a, loc_b,
):
    me_h = lax.axis_index("head")
    me_c = lax.axis_index("ctx")
    my_q = pl.ds(pl.multiple_of(me_h * QROWS, QROWS), QROWS)
    own_copies = [
        pltpu.make_async_copy(ug_hbm.at[0, me_h], urecv.at[0, me_h], loc.at[0]),
        pltpu.make_async_copy(ug_hbm.at[1, me_h], urecv.at[1, me_h], loc.at[1]),
        pltpu.make_async_copy(iqg_hbm.at[me_h], iqg_out.at[my_q], loc.at[2]),
        pltpu.make_async_copy(wg_hbm.at[me_h], wrecv.at[me_h], loc.at[3]),
    ]
    for c in own_copies:
        c.start()
    start_barrier(me_h, me_c)
    sends = []

    def send_sums(q):
        for o in (1, 7, 3, 5, 2, 6, 4):
            h = lax.rem(me_h + o, NH)
            s = remote(
                ug_hbm.at[q, h], urecv.at[q, me_h], u_send.at[q * NH + o], u_recv.at[q * NH + o], (h, me_c)
            )
            s.start()
            sends.append(s)

    def take_sums(q):
        own_copies[q].wait()
        for o in range(1, NH):
            h = lax.rem(me_h + NH - o, NH)
            remote(
                ug_hbm.at[q, h], urecv.at[q, h], u_send.at[q * NH + o], u_recv.at[q * NH + o], (h, me_c)
            ).wait_recv()

    def send_blocks(q):
        for j in range(SETB):
            rows = slice(j * HB, (j + 1) * HB)
            acc = urecv[q, 0, rows, :]
            for h in range(1, NH):
                acc = acc + urecv[q, h, rows, :]
            sums[q, j] = acc
        sums[q, SETB] = jnp.zeros((HB, 128), jnp.float32)
        for o in range(1, NC + 1):
            c = lax.rem(me_c + o, NC)
            value = sums[q, tab_s[8 + me_h, c]]
            if o < NC:
                slots[q, o] = value
                s = remote(
                    slots.at[q, o], brecv.at[q, me_c], b_send.at[q * NC + o], b_recv.at[q * NC + o], (me_h, c)
                )
                s.start()
                sends.append(s)
            else:
                brecv[q, me_c] = value

    def take_blocks(q):
        for o in range(1, NC):
            c = lax.rem(me_c + NC - o, NC)
            remote(
                slots.at[q, o], brecv.at[q, c], b_send.at[q * NC + o], b_recv.at[q * NC + o], (me_h, c)
            ).wait_recv()
        for r in range(NC):
            at = (q * NC + r) * HB
            own[at : at + HB, :] = brecv[q, r].astype(own.dtype)

    rows = NC * HB
    send_sums(0)
    take_sums(0)
    send_sums(1)
    send_blocks(0)
    take_blocks(0)
    ga = gather_sets([(own, kg_out, 0, rows)], me_h, me_c, g_send, g_recv, loc_a)
    next(ga)
    take_sums(1)
    send_blocks(1)
    for o in range(1, NH):
        h = lax.rem(me_h + o, NH)
        s = remote(iqg_hbm.at[h], iqg_out.at[my_q], i_send.at[o], i_recv.at[o], (h, me_c))
        s.start()
        sends.append(s)
        s = remote(wg_hbm.at[h], wrecv.at[me_h], w_send.at[o], w_recv.at[o], (h, me_c))
        s.start()
        sends.append(s)
    next(ga)
    take_blocks(1)
    gb = gather_sets([(own, kg_out, rows, rows)], me_h, me_c, h_send, h_recv, loc_b)
    next(gb)
    finish(ga, gb)
    for o in range(1, NH):
        h = lax.rem(me_h + NH - o, NH)
        remote(
            iqg_hbm.at[h], iqg_out.at[pl.ds(pl.multiple_of(h * QROWS, QROWS), QROWS)],
            i_send.at[o], i_recv.at[o], (h, me_c),
        ).wait_recv()
        remote(wg_hbm.at[h], wrecv.at[h], w_send.at[o], w_recv.at[o], (h, me_c)).wait_recv()
    own_copies[2].wait()
    own_copies[3].wait()
    acc = wrecv[0]
    for h in range(1, NH):
        acc = acc + wrecv[h]
    wg_out[...] = acc
    for s in sends:
        s.wait_send()


SENT = jnp.bfloat16


def give_back(tab, ug, iqg, wg):
    f32 = jnp.float32
    any_spec = pl.BlockSpec(memory_space=ANY)
    return pl.pallas_call(
        return_kernel,
        name="give_back",
        out_shape=(
            jax.ShapeDtypeStruct((NH * QROWS, 1024), f32),
            jax.ShapeDtypeStruct((8, 128), f32),
            jax.ShapeDtypeStruct((NH, NC * BLK, 128), SENT),
        ),
        in_specs=[pl.BlockSpec(memory_space=pltpu.SMEM)] + [any_spec] * 3,
        out_specs=(any_spec, pl.BlockSpec(memory_space=VM), any_spec),
        scratch_shapes=[
            VM((2, NH, SETT // 2, 128), f32),
            VM((2, SETB + 1, HB, 128), f32),
            VM((2, NC, HB, 128), f32),
            VM((2, NC, HB, 128), f32),
            VM((NC * BLK, 128), SENT),
            VM((NH, 8, 128), f32),
            DMA((2 * NH,)), DMA((2 * NH,)), DMA((NH,)), DMA((NH,)), DMA((NH,)), DMA((NH,)),
            DMA((2 * NC,)), DMA((2 * NC,)),
            DMA((9,)), DMA((9,)), DMA((9,)), DMA((9,)), DMA((4,)), DMA((1,)), DMA((1,)),
        ],
        compiler_params=pltpu.CompilerParams(
            collective_id=1, has_side_effects=True, vmem_limit_bytes=60 << 20
        ),
    )(tab, ug, iqg, wg)


def scatter_kernel(asked_s, kg_ref, out_ref):
    out_ref[...] = jnp.zeros(out_ref.shape, jnp.float32)

    def one(i, carry):
        h = lax.shift_right_logical(i, 4)
        r = lax.bitwise_and(i, 15)
        b = asked_s[r, h]
        for q in range(2):
            rows = pl.ds(pl.multiple_of(b * BLK + q * HB, HB), HB)
            part = kg_ref[h, pl.ds(pl.multiple_of((q * NC + r) * HB, HB), HB), :]
            out_ref[rows, :] = out_ref[rows, :] + part.astype(jnp.float32)
        return carry

    lax.fori_loop(0, NH * NC, one, 0)


def scatter(asked, kg, tokens):
    return pl.pallas_call(
        scatter_kernel,
        name="scatter",
        out_shape=jax.ShapeDtypeStruct((tokens, 128), jnp.float32),
        in_specs=[pl.BlockSpec(memory_space=pltpu.SMEM), pl.BlockSpec(memory_space=VM)],
        out_specs=pl.BlockSpec(memory_space=VM),
        compiler_params=pltpu.CompilerParams(vmem_limit_bytes=60 << 20),
    )(asked, kg)


def shards(main_query, latent, index_query, index_key, index_weight, selected, lengths, cotangent):
    sel_t = selected.T
    req, tab = make_plan(sel_t)
    kt, ik, mq, iq, w, asked = fetch(
        tab, req, latent.T, index_key.reshape(-1, BLK, WIDTH), main_query, index_query, index_weight.T
    )
    ug, iqg, wg = core(tab, kt, ik, mq, iq, w, sel_t, lengths[None, :], cotangent[None, :])
    query_grad, weight_grad, kg = give_back(tab, ug, iqg, wg)
    key_grad = scatter(asked, kg, latent.shape[0])
    return query_grad, weight_grad.T, key_grad


def solution(mesh):
    return jax.shard_map(
        shards,
        mesh=mesh,
        in_specs=(
            P("ctx", "head"),
            P("ctx", None),
            P("ctx", "head"),
            P("ctx", None),
            P("ctx", "head"),
            P("ctx", None),
            P("ctx"),
            P("ctx"),
        ),
        out_specs=(P("ctx", "head"), P("ctx", "head"), P("ctx", None)),
        check_vma=False,
    )
```

time: 272 us -> 220 us (0.81); the launches traced: 268 us -> 220 us
  Pallas kernels: 248 us -> 218 us
  local copies, waits for them, and re-layouts: 19.3 us -> 1.39 us
    unnamed x32 -> x6, local copies, waits for them, and re-layouts: 19.3 us -> 1.39 us
    pallas_call x1, Pallas kernels: 112 us -> 100 us  [fetch(): pl.pallas_call(fetch_kernel, name='fetch', out_shape=(jax.ShapeDtypeStruc...]
    pallas_call x1, Pallas kernels: 85.1 us -> 74 us  [give_back(): pl.pallas_call(return_kernel, name='give_back', out_shape=(jax.ShapeDtype...]
    pallas_call x1, Pallas kernels: 45.6 us -> 36.4 us  [core(): pl.pallas_call(core_kernel, name='core', out_shape=(jax.ShapeDtypeStruct(...]
where the time goes in v2:
time: 220 us
  Pallas kernels  218 us (99%)
    pallas_call x1, Pallas kernels, fetch(): pl.pallas_call(fetch_kernel, name='fetch', out_shape=(jax.ShapeDtypeStruc...  100 us
    pallas_call x1, Pallas kernels, give_back(): pl.pallas_call(return_kernel, name='give_back', out_shape=(jax.ShapeDtype...  74 us
    pallas_call x1, Pallas kernels, core(): pl.pallas_call(core_kernel, name='core', out_shape=(jax.ShapeDtypeStruct(...  36.4 us
    pallas_call x1, Pallas kernels, scatter(): pl.pallas_call(scatter_kernel, name='scatter', out_shape=jax.ShapeDtypeSt...  5.35 us

profile of v2, /device:TPU:0, one launch (start us, length us, event | category | flops | bytes accessed | tf_op | source)
XLA Modules:
  0.0 220.0 jit_solution(10263700770467762066)
XLA Ops:
  0.6 2.2 plan.1
  2.8 100.0 %fetch.1 = (bf16[8,576,512]{2,1,0:T(8,128)(2,1)}, bf16[8,512,128]{2,1,0:T(8,128)(2,1)}, bf16[8,16,9216]{2,1,0:T(8,128)(2,1)}, bf16[8,16,1024]{2,1,0:T(8,128)(2,1...) custom-call(s32[16,128]{1,0:T(8,128)} %get-tuple-element.17.tab_s, s32[16,8,128]{2,1,0:T(8,128)} %get-tuple-element.18.req, ...), custom_call_target="tpu_custom_call" | custom-call | tf_op jit(solution)/shard_map/fetch/pallas_call | solution.py:348
  102.8 36.4 %core.1 = (f32[2,8,256,128]{3,2,1,0:T(8,128)}, f32[8,16,1024]{2,1,0:T(8,128)}, f32[8,8,128]{2,1,0:T(8,128)}) custom-call(s32[16,128]{1,0:T(8,128)} %get-tuple-element.17.tab_s, bf16[8,576,512]{2,1,0:T(8,128)(2,1)} %get-tuple-element.19.kt_hbm, bf16[8,512,128]{2,1,0:T(8,128)(2,1)} %get-tuple-element.20.ik_hbm, bf16[8,16,9216]{2,1,0:T(8,128)(2,1)} %get-tuple-element.21.mq_ref, ...), custom_call_target="tpu_custom_call" | custom-call | tf_op jit(solution)/shard_map/core/pallas_call | solution.py:583
  139.2 74.0 %give_back.1 = (f32[128,1024]{1,0:T(8,128)}, f32[8,128]{1,0:T(8,128)}, bf16[8,1024,128]{2,1,0:T(8,128)(2,1)}) custom-call(s32[16,128]{1,0:T(8,128)} %get-tuple-element.17.tab_s, f32[2,8,256,128]{3,2,1,0:T(8,128)} %get-tuple-element.24.ug_hbm, f32[8,16,1024]{2,1,0:T(8,128)} %get-tuple-element.25.iqg_hbm, f32[8,8,128]{2,1,0:T(8,128)} %get-tuple-element.26.wg_hbm), custom_call_target="tpu_custom_call" | custom-call | tf_op jit(solution)/shard_map/give_back/pallas_call | solution.py:740
  213.2 0.0 copy-start
  213.2 0.0 copy-start.1
  213.2 5.4 %scatter.1 = f32[8192,128]{1,0:T(8,128)} custom-call(s32[16,128]{1,0:T(8,128)} %get-tuple-element.29.asked_s, bf16[8,1024,128]{2,1,0:T(8,128)(2,1)} %get-tuple-element.30.kg_ref), custom_call_target="tpu_custom_call" | custom-call | tf_op jit(solution)/shard_map/scatter/pallas_call | solution.py:784
  218.6 0.0 copy-done
  218.6 0.8 copy.13
  219.4 0.0 copy-done.1
  219.4 0.6 copy.14
Async XLA Ops:
  213.2 5.4 %copy-start = (f32[128,1024]{1,0:T(8,128)S(1)}, f32[128,1024]{1,0:T(8,128)}, u32[]{:S(2)}) copy-start(f32[128,1024]{1,0:T(8,128)} %get-tuple-element.34) | copy-start | bytes 1572868
  213.2 6.2 %copy-start.1 = (f32[8,128]{1,0:T(8,128)S(1)}, f32[8,128]{1,0:T(8,128)}, u32[]{:S(2)}) copy-start(f32[8,128]{1,0:T(8,128)} %get-tuple-element.28) | copy-start | bytes 12292

commit v3 on v2

--- a/solution.py
+++ b/solution.py
@@ -80,7 +80,7 @@
     def copy(n, i, h, which, device, first=False):
         own, out, _, _ = pieces[n]
         start, rows = part(n, which)
-        dst = out.at[h, pl.ds(start, rows)]
+        dst = out(h, start, rows)
         src = own.at[pl.ds(start, rows)] if first else dst
         return remote(src, dst, ssem.at[i * count + n], rsem.at[i * count + n], device)
 
@@ -95,7 +95,7 @@
             copy(n, i, h, which, device).wait_recv()
 
     locals_ = [
-        pltpu.make_async_copy(own.at[pl.ds(start, rows)], out.at[me_h, pl.ds(start, rows)], lsem.at[n])
+        pltpu.make_async_copy(own.at[pl.ds(start, rows)], out(me_h, start, rows), lsem.at[n])
         for n, (own, out, start, rows) in enumerate(pieces)
     ]
     for c in locals_:
@@ -207,16 +207,22 @@
     )(sel_t)
 
 
-SPLIT = HALF // 2
-
-
-def fetch_kernel(
-    tab_s, req, lat_hbm, ik_hbm, mq_hbm, iq_hbm, w_hbm,
-    kt_out, ik_out, mq_out, iq_out, w_out, asked_out,
+SPLIT = SLOT // 2
+FIRST = SPLIT - BLK
+AUG = LAT + QROWS
+TILE = 256
+
+
+def forward_kernel(
+    tab_s, req, sel_ref, len_ref, cot_ref, lat_hbm, ik_hbm, mq_hbm, iq_hbm, w_hbm,
+    grad_ref, iqr_ref, wrow_ref, asked_out, ik_out,
     lat_v, ik_v, stage, recv_a, recv_b, own, own_ik, asked, asked_s,
+    kt_ref, ik_ref, mq_ref, iq_ref, w_ref,
+    sa_ref, sb_ref, ma_ref, mb_ref, qt_ref, bias_ref, tgt_ref, idx_ref, meta_ref, selb_ref, wb_ref,
     q_send, q_recv, i_send, i_recv, w_send, w_recv, r_send, r_recv, b_send, b_recv, c_send, c_recv,
     g_send, g_recv, h_send, h_recv, loc, loc_a, loc_b, l_sem,
 ):
+    f32, bf = jnp.float32, jnp.bfloat16
     me_h = lax.axis_index("head")
     me_c = lax.axis_index("ctx")
     loads = [pltpu.make_async_copy(ik_hbm, ik_v, loc.at[1])] + [
@@ -225,14 +231,13 @@
     ]
     for c in loads:
         c.start()
-    my_q = pl.ds(pl.multiple_of(me_h * QROWS, QROWS), QROWS)
-    own_copies = [
-        pltpu.make_async_copy(mq_hbm.at[my_q], mq_out.at[me_h], loc.at[2]),
-        pltpu.make_async_copy(iq_hbm.at[my_q], iq_out.at[me_h], loc.at[3]),
-        pltpu.make_async_copy(w_hbm, w_out.at[me_h], loc.at[4]),
-    ]
-    for c in own_copies:
-        c.start()
+    mine = pl.ds(pl.multiple_of(me_h * QROWS, QROWS), QROWS)
+    own_mq = pltpu.make_async_copy(mq_hbm.at[mine], mq_ref.at[me_h], loc.at[2])
+    own_iq = pltpu.make_async_copy(iq_hbm.at[mine], iq_ref.at[me_h], loc.at[3])
+    own_w = pltpu.make_async_copy(w_hbm, w_ref.at[me_h], loc.at[4])
+    own_mq.start()
+    own_iq.start()
+    own_w.start()
     start_barrier(me_h, me_c)
     sends = []
     own_req = pltpu.make_async_copy(req.at[me_c], asked.at[me_c], loc.at[6])
@@ -243,18 +248,23 @@
         s.start()
         sends.append(s)
 
+    def query_copy(o, back=False):
+        h = lax.rem(me_h + (NH - o if back else o), NH)
+        rows = pl.ds(0, QROWS) if back else pl.ds(pl.multiple_of(h * QROWS, QROWS), QROWS)
+        return remote(mq_hbm.at[rows], mq_ref.at[h if back else me_h], q_send.at[o], q_recv.at[o], (h, me_c))
+
     def send_queries(o):
+        s = query_copy(o)
+        s.start()
+        sends.append(s)
+
+    for o in range(1, NH):
         h = lax.rem(me_h + o, NH)
         rows = pl.ds(pl.multiple_of(h * QROWS, QROWS), QROWS)
-        for src, dst, ss, rs in (
-            (mq_hbm.at[rows], mq_out, q_send, q_recv),
-            (iq_hbm.at[rows], iq_out, i_send, i_recv),
-            (w_hbm, w_out, w_send, w_recv),
-        ):
+        for src, dst, ss, rs in ((iq_hbm.at[rows], iq_ref, i_send, i_recv), (w_hbm, w_ref, w_send, w_recv)):
             s = remote(src, dst.at[me_h], ss.at[o], rs.at[o], (h, me_c))
             s.start()
             sends.append(s)
-
     for o in (2, 6, 4):
         send_queries(o)
     own_req.wait()
@@ -276,132 +286,34 @@
         b = asked_s[r, me_h]
         odd = jnp.full((HALF, 128), lax.bitwise_and(b, 1), jnp.int32) == 1
         pair = lax.shift_right_logical(b, 1)
-        top = lat_v[pair, 0:HALF, :].astype(jnp.float32)
-        bot = lat_v[pair, HALF:LAT, :].astype(jnp.float32)
+        top = lat_v[pair, 0:HALF, :].astype(f32)
+        bot = lat_v[pair, HALF:LAT, :].astype(f32)
         packed = jnp.where(
             first, jnp.where(odd, roll64(top), top), jnp.where(odd, bot, roll64(bot))
-        ).astype(jnp.bfloat16)
+        ).astype(bf)
         keys = ik_v[b]
         if o < NC:
-            stage[o, 0:HALF, :] = packed
-            stage[o, HALF:SLOT, :] = keys
+            stage[o, 0:BLK, :] = keys
+            stage[o, BLK:SLOT, :] = packed
             s = remote(stage.at[o, lower], recv_a.at[me_c], b_send.at[o], b_recv.at[o], (me_h, r))
             s.start()
             sends.append(s)
             late.append(remote(stage.at[o, upper], recv_b.at[me_c], c_send.at[o], c_recv.at[o], (me_h, r)))
         else:
-            recv_a[me_c] = packed[0:SPLIT]
-            recv_b[me_c, 0 : HALF - SPLIT, :] = packed[SPLIT:HALF]
-            recv_b[me_c, HALF - SPLIT : SLOT - SPLIT, :] = keys
+            recv_a[me_c, 0:BLK, :] = keys
+            recv_a[me_c, BLK:SPLIT, :] = packed[0:FIRST]
+            recv_b[me_c] = packed[FIRST:HALF]
     for s in late:
         s.start()
         sends.append(s)
     owners = [tab_s[1, me_h * SETB + j] for j in range(SETB)]
 
-    def merge(lo, hi, recv):
-        here = iota((hi - lo, 128), 1) < 64
-        for i in range(SETB // 2):
-            cols = slice(i * 128, (i + 1) * 128)
-            a = recv[owners[2 * i], 0 : hi - lo, :].astype(jnp.float32)
-            b = recv[owners[2 * i + 1], 0 : hi - lo, :].astype(jnp.float32)
-            own[lo:hi, cols] = jnp.where(here, a, roll64(b)).astype(jnp.bfloat16)
-            own[HALF + lo : HALF + hi, cols] = jnp.where(here, roll64(a), b).astype(jnp.bfloat16)
-
-    for o in range(1, NC):
-        c = lax.rem(me_c + NC - o, NC)
-        remote(stage.at[o, lower], recv_a.at[c], b_send.at[o], b_recv.at[o], (me_h, c)).wait_recv()
-    merge(0, SPLIT, recv_a)
-    ga = gather_sets(
-        [(own, kt_out, 0, SPLIT), (own, kt_out, HALF, SPLIT)], me_h, me_c, g_send, g_recv, loc_a
-    )
-    next(ga)
-    for o in range(1, NC):
-        c = lax.rem(me_c + NC - o, NC)
-        remote(stage.at[o, upper], recv_b.at[c], c_send.at[o], c_recv.at[o], (me_h, c)).wait_recv()
-    merge(SPLIT, HALF, recv_b)
-    for j in range(SETB):
-        own_ik[j * BLK : (j + 1) * BLK, :] = recv_b[owners[j], HALF - SPLIT : SLOT - SPLIT, :]
-    gb = gather_sets(
-        [(own, kt_out, SPLIT, HALF - SPLIT), (own, kt_out, HALF + SPLIT, HALF - SPLIT), (own_ik, ik_out, 0, SETT)],
-        me_h, me_c, h_send, h_recv, loc_b,
-    )
-    next(gb)
-    for o in (1, 7, 3, 5):
-        send_queries(o)
-    finish(ga, gb)
+    own_w.wait()
+    own_iq.wait()
     for o in range(1, NH):
         h = lax.rem(me_h + NH - o, NH)
-        rows = pl.ds(0, QROWS)
-        remote(mq_hbm.at[rows], mq_out.at[h], q_send.at[o], q_recv.at[o], (h, me_c)).wait_recv()
-        remote(iq_hbm.at[rows], iq_out.at[h], i_send.at[o], i_recv.at[o], (h, me_c)).wait_recv()
-        remote(w_hbm, w_out.at[h], w_send.at[o], w_recv.at[o], (h, me_c)).wait_recv()
-    for c in own_copies:
-        c.wait()
-    for s in sends:
-        s.wait_send()
-
-
-def fetch(tab, req, lat_t, index_key, main_query, index_query, weight_t):
-    any_spec = pl.BlockSpec(memory_space=ANY)
-    vm_spec = pl.BlockSpec(memory_space=VM)
-    bf, i32 = jnp.bfloat16, jnp.int32
-    return pl.pallas_call(
-        fetch_kernel,
-        name="fetch",
-        out_shape=(
-            jax.ShapeDtypeStruct((NH, LAT, SETT), bf),
-            jax.ShapeDtypeStruct((NH, SETT, 128), bf),
-            jax.ShapeDtypeStruct((NH, QROWS, main_query.shape[1]), bf),
-            jax.ShapeDtypeStruct((NH, QROWS, index_query.shape[1]), bf),
-            jax.ShapeDtypeStruct((NH, 8, 128), jnp.float32),
-            jax.ShapeDtypeStruct((16, 128), i32),
-        ),
-        in_specs=[pl.BlockSpec(memory_space=pltpu.SMEM), vm_spec] + [any_spec] * 5,
-        out_specs=(any_spec,) * 5 + (vm_spec,),
-        scratch_shapes=[
-            VM((lat_t.shape[1] // 128, LAT, 128), bf),
-            VM(index_key.shape, bf),
-            VM((NC, SLOT, 128), bf),
-            VM((NC, SPLIT, 128), bf),
-            VM((NC, SLOT - SPLIT, 128), bf),
-            VM((LAT, SETT), bf),
-            VM((SETT, 128), bf),
-            VM((NC, 8, 128), i32),
-            pltpu.SMEM((16, 128), i32),
-            DMA((NH,)), DMA((NH,)), DMA((NH,)), DMA((NH,)), DMA((NH,)), DMA((NH,)),
-            DMA((NC,)), DMA((NC,)), DMA((NC,)), DMA((NC,)), DMA((NC,)), DMA((NC,)),
-            DMA((18,)), DMA((18,)), DMA((27,)), DMA((27,)), DMA((9,)), DMA((3,)), DMA((3,)),
-            DMA((lat_t.shape[1] // 128,)),
-        ],
-        compiler_params=pltpu.CompilerParams(
-            collective_id=0, has_side_effects=True, vmem_limit_bytes=60 << 20
-        ),
-    )(tab, req, lat_t, index_key, main_query, index_query, weight_t)
-
-
-AUG = LAT + QROWS
-TILE = 256
-
-
-def core_kernel(
-    tab_s, kt_hbm, ik_hbm, mq_ref, iq_ref, w_ref, sel_ref, len_ref, cot_ref,
-    ug_ref, iqg_ref, wg_ref,
-    kt_ref, ik_ref, sa_ref, sb_ref, ma_ref, mb_ref, qt_ref, pre_ref, ea_ref, eb_ref, bias_ref, tgt_ref, idx_ref,
-    grad_ref, meta_ref, wq_ref, selb_ref, wb_ref, iqr_ref, wcol_ref, iqg_acc, sem_k, sem_i,
-):
-    me = lax.axis_index("head")
-    mine = pl.ds(pl.multiple_of(me * QROWS, QROWS), QROWS)
-    f32, bf = jnp.float32, jnp.bfloat16
-    i_loads, k_loads = [], []
-    for h in range(NH):
-        i_loads.append(pltpu.make_async_copy(ik_hbm.at[h], ik_ref.at[pl.ds(h * SETT, SETT)], sem_i.at[h]))
-        k_loads.append(
-            pltpu.make_async_copy(
-                kt_hbm.at[h], kt_ref.at[pl.ds(0, LAT), pl.ds(h * SETT, SETT)], sem_k.at[h]
-            )
-        )
-    for c in i_loads + k_loads:
-        c.start()
+        remote(iq_hbm.at[pl.ds(0, QROWS)], iq_ref.at[h], i_send.at[o], i_recv.at[o], (h, me_c)).wait_recv()
+        remote(w_hbm, w_ref.at[h], w_send.at[o], w_recv.at[o], (h, me_c)).wait_recv()
     top = sel_ref.shape[0]
     meta_ref[...] = jnp.zeros((128, 128), f32)
     meta_ref[0:top, :] = sel_ref[...].astype(f32)
@@ -410,6 +322,7 @@
     meta_ref[64 : 64 + IHEADS, :] = w_ref[...].reshape(IHEADS, 128)
     meta_ref[...] = meta_ref[...].T
     row = meta_ref[mine, :]
+    wrow_ref[...] = row
     for i in range(top):
         selb_ref[i] = jnp.broadcast_to(row[:, i : i + 1], (QROWS, 128))
     limit = jnp.broadcast_to(row[:, top : top + 1], (QROWS, 128))
@@ -433,12 +346,57 @@
         return carry
 
     lax.fori_loop(0, UNION // 128, mask_tile, 0)
-
     for h in range(NH):
         for k in range(8):
             iqr_ref[(h * 8 + k) * QROWS : (h * 8 + k + 1) * QROWS, :] = iq_ref[h, :, k * 128 : (k + 1) * 128]
-    for c in i_loads:
-        c.wait()
+    hot = jnp.where(iota((QROWS, QROWS), 0) == iota((QROWS, QROWS), 1), 1.0, 0.0).astype(bf)
+    per = mq_ref.shape[2] // LAT
+    for k in range(per):
+        qt_ref[k * QROWS : (k + 1) * QROWS, LAT:AUG] = hot
+
+    def merge(recv, skip, lo, hi):
+        here = iota((hi - lo, 128), 1) < 64
+        for i in range(SETB // 2):
+            cols = slice(i * 128, (i + 1) * 128)
+            a = recv[owners[2 * i], skip : skip + hi - lo, :].astype(f32)
+            b = recv[owners[2 * i + 1], skip : skip + hi - lo, :].astype(f32)
+            own[lo:hi, cols] = jnp.where(here, a, roll64(b)).astype(bf)
+            own[HALF + lo : HALF + hi, cols] = jnp.where(here, roll64(a), b).astype(bf)
+
+    def kt_of(h, start, rows):
+        return kt_ref.at[pl.ds(start, rows), pl.ds(pl.multiple_of(h * SETT, SETT), SETT)]
+
+    def ik_of(h, start, rows):
+        return ik_ref.at[h, pl.ds(start, rows)]
+
+    for o in range(1, NC):
+        c = lax.rem(me_c + NC - o, NC)
+        remote(stage.at[o, lower], recv_a.at[c], b_send.at[o], b_recv.at[o], (me_h, c)).wait_recv()
+    merge(recv_a, BLK, 0, FIRST)
+    for j in range(SETB):
+        own_ik[j * BLK : (j + 1) * BLK, :] = recv_a[owners[j], 0:BLK, :]
+    ga = gather_sets(
+        [(own_ik, ik_of, 0, SETT), (own, kt_of, 0, FIRST), (own, kt_of, HALF, FIRST)],
+        me_h, me_c, g_send, g_recv, loc_a,
+    )
+    next(ga)
+    for o in range(1, NC):
+        c = lax.rem(me_c + NC - o, NC)
+        remote(stage.at[o, upper], recv_b.at[c], c_send.at[o], c_recv.at[o], (me_h, c)).wait_recv()
+    merge(recv_b, 0, FIRST, HALF)
+    next(ga)
+    gb = gather_sets(
+        [(own, kt_of, FIRST, HALF - FIRST), (own, kt_of, HALF + FIRST, HALF - FIRST)],
+        me_h, me_c, h_send, h_recv, loc_b,
+    )
+    next(gb)
+    next(ga)
+    next(gb)
+    next(ga)
+    next(gb)
+    for o in (1, 7, 3, 5):
+        send_queries(o)
+    finish(ga)
 
     def index_chunk(i, carry):
         cols = pl.ds(pl.multiple_of(i * SETT, SETT), SETT)
@@ -446,28 +404,33 @@
         for b in range(4):
             rows = slice(b * 256, (b + 1) * 256)
             pre = lax.dot_general(
-                iqr_ref[rows, :], ik_ref[cols, :], (((1,), (1,)), ((), ())), preferred_element_type=f32
+                iqr_ref[rows, :], ik_ref[i], (((1,), (1,)), ((), ())), preferred_element_type=f32
             )
-            pre_ref[rows, cols] = pre
             for j in range(16):
                 w = jnp.concatenate([wb_ref[b * 16 + j]] * (SETT // 128), axis=1)
                 acc = acc + w * jnp.maximum(pre[j * QROWS : (j + 1) * QROWS, :], 0.0)
         idx_ref[:, cols] = acc + bias_ref[:, cols]
         return carry
 
-    lax.fori_loop(0, NH, index_chunk, 0)
-
+    lax.fori_loop(0, NH // 2, index_chunk, 0)
+    next(gb)
+    lax.fori_loop(NH // 2, NH, index_chunk, 0)
+    keys_out = pltpu.make_async_copy(ik_ref, ik_out, loc.at[5])
+    keys_out.start()
+    v = idx_ref[...]
+    e = jnp.exp(v - jnp.max(v, axis=1, keepdims=True))
+    idx_ref[...] = e / jnp.sum(e, axis=1, keepdims=True)
     tgt_ref[...] = jnp.zeros((QROWS, UNION), f32)
-    per = mq_ref.shape[2] // LAT
-    hot = jnp.where(iota((QROWS, QROWS), 0) == iota((QROWS, QROWS), 1), 1.0, 0.0).astype(bf)
-    for k in range(per):
-        qt_ref[k * QROWS : (k + 1) * QROWS, LAT:AUG] = hot
-    for c in k_loads:
-        c.wait()
+    finish(gb)
 
     def load_queries(g):
         for k in range(per):
             qt_ref[k * QROWS : (k + 1) * QROWS, 0:LAT] = mq_ref[g, :, k * LAT : (k + 1) * LAT]
+
+    def arrive(n):
+        o = lax.rem(2 * n, NH) + lax.div(n, NH // 2)
+        query_copy(o, True).wait_recv()
+        load_queries(lax.rem(me_h + NH - o, NH))
 
     def score_tile(t, s_ref, m_ref):
         cols = slice(t * TILE, (t + 1) * TILE)
@@ -506,27 +469,94 @@
                 add_up(recips, s_ref, k - 7)
                 recips = []
 
-    load_queries(0)
+    own_mq.wait()
+    load_queries(me_h)
     for t in range(UNION // TILE):
         score_tile(t, sa_ref, ma_ref)
 
     def two_groups(i, carry):
-        load_queries(2 * i + 1)
+        arrive(2 * i + 1)
         both(sa_ref, ma_ref, sb_ref, mb_ref)
-        load_queries(2 * i + 2)
+        arrive(2 * i + 2)
         both(sb_ref, mb_ref, sa_ref, ma_ref)
         return carry
 
     lax.fori_loop(0, NH // 2 - 1, two_groups, 0)
-    load_queries(NH - 1)
+    arrive(NH - 1)
     both(sa_ref, ma_ref, sb_ref, mb_ref)
     both(sb_ref, mb_ref, None, None)
-
-    v = idx_ref[...]
-    e = jnp.exp(v - jnp.max(v, axis=1, keepdims=True))
-    chosen = e / jnp.sum(e, axis=1, keepdims=True)
-    grad_ref[...] = cot * (chosen - tgt_ref[...] * (1.0 / HEADS))
-
+    grad_ref[...] = cot * (idx_ref[...] - tgt_ref[...] * (1.0 / HEADS))
+    keys_out.wait()
+    for s in sends:
+        s.wait_send()
+
+
+def forward(tab, req, sel_t, lengths, cot, lat_t, index_key, main_query, index_query, weight_t):
+    any_spec = pl.BlockSpec(memory_space=ANY)
+    vm_spec = pl.BlockSpec(memory_space=VM)
+    f32, bf, i32 = jnp.float32, jnp.bfloat16, jnp.int32
+    rows = IHEADS * QROWS
+    return pl.pallas_call(
+        forward_kernel,
+        name="forward",
+        out_shape=(
+            jax.ShapeDtypeStruct((QROWS, UNION), f32),
+            jax.ShapeDtypeStruct((rows, 128), bf),
+            jax.ShapeDtypeStruct((QROWS, 128), f32),
+            jax.ShapeDtypeStruct((16, 128), i32),
+            jax.ShapeDtypeStruct((NH, SETT, 128), bf),
+        ),
+        in_specs=[pl.BlockSpec(memory_space=pltpu.SMEM)] + [vm_spec] * 4 + [any_spec] * 5,
+        out_specs=(vm_spec,) * 4 + (any_spec,),
+        scratch_shapes=[
+            VM((lat_t.shape[1] // 128, LAT, 128), bf),
+            VM(index_key.shape, bf),
+            VM((NC, SLOT, 128), bf),
+            VM((NC, SPLIT, 128), bf),
+            VM((NC, SLOT - SPLIT, 128), bf),
+            VM((LAT, SETT), bf),
+            VM((SETT, 128), bf),
+            VM((NC, 8, 128), i32),
+            pltpu.SMEM((16, 128), i32),
+            VM((AUG, UNION), bf),
+            VM((NH, SETT, 128), bf),
+            VM((NH, QROWS, main_query.shape[1]), bf),
+            VM((NH, QROWS, index_query.shape[1]), bf),
+            VM((NH, 8, 128), f32),
+            VM((256, UNION), f32),
+            VM((256, UNION), f32),
+            VM((256, 128), f32),
+            VM((256, 128), f32),
+            VM((256, AUG), bf),
+            VM((QROWS, UNION), f32),
+            VM((QROWS, UNION), f32),
+            VM((QROWS, UNION), f32),
+            VM((128, 128), f32),
+            VM((32, QROWS, 128), f32),
+            VM((IHEADS, QROWS, 128), f32),
+            DMA((NH,)), DMA((NH,)), DMA((NH,)), DMA((NH,)), DMA((NH,)), DMA((NH,)),
+            DMA((NC,)), DMA((NC,)), DMA((NC,)), DMA((NC,)), DMA((NC,)), DMA((NC,)),
+            DMA((27,)), DMA((27,)), DMA((18,)), DMA((18,)), DMA((9,)), DMA((3,)), DMA((3,)),
+            DMA((lat_t.shape[1] // 128,)),
+        ],
+        compiler_params=pltpu.CompilerParams(
+            collective_id=0, has_side_effects=True, vmem_limit_bytes=60 << 20
+        ),
+    )(tab, req, sel_t, lengths, cot, lat_t, index_key, main_query, index_query, weight_t)
+
+
+def back_kernel(
+    grad_ref, iqr_ref, row_ref, ik_ref,
+    ug_ref, iqg_ref, wg_ref,
+    ea_ref, eb_ref, wq_ref, wb_ref, wcol_ref, iqg_acc,
+):
+    me = lax.axis_index("head")
+    mine = pl.ds(pl.multiple_of(me * QROWS, QROWS), QROWS)
+    f32, bf = jnp.float32, jnp.bfloat16
+    lane = iota((QROWS, 128), 1)
+    row = row_ref[...]
+    for j in range(IHEADS):
+        wb_ref[j] = jnp.broadcast_to(row[:, 64 + j : 65 + j], (QROWS, 128))
     wcol_ref[...] = jnp.zeros(wcol_ref.shape, f32)
     iqg_acc[...] = jnp.zeros(iqg_acc.shape, f32)
     iq_t = iqr_ref[...].T
@@ -534,22 +564,25 @@
     def edges(h, e_ref):
         cols = pl.ds(pl.multiple_of(h * SETT, SETT), SETT)
         grad = grad_ref[:, cols]
-        for j in range(IHEADS):
-            rows = slice(j * QROWS, (j + 1) * QROWS)
-            pre = pre_ref[rows, cols]
-            w = jnp.concatenate([wb_ref[j]] * (SETT // 128), axis=1)
-            part = jnp.maximum(pre, 0.0) * grad
-            wcol_ref[j] = wcol_ref[j] + sum(part[:, t * 128 : (t + 1) * 128] for t in range(SETT // 128))
-            e_ref[rows, :] = jnp.where(pre > 0.0, grad * w, 0.0).astype(bf)
+        for b in range(4):
+            pre_b = lax.dot_general(
+                iqr_ref[b * 256 : (b + 1) * 256, :], ik_ref[h], (((1,), (1,)), ((), ())), preferred_element_type=f32
+            )
+            for q in range(16):
+                j = b * 16 + q
+                pre = pre_b[q * QROWS : (q + 1) * QROWS, :]
+                w = jnp.concatenate([wb_ref[j]] * (SETT // 128), axis=1)
+                part = jnp.maximum(pre, 0.0) * grad
+                wcol_ref[j] = wcol_ref[j] + sum(part[:, t * 128 : (t + 1) * 128] for t in range(SETT // 128))
+                e_ref[j * QROWS : (j + 1) * QROWS, :] = jnp.where(pre > 0.0, grad * w, 0.0).astype(bf)
 
     def products(h, e_ref):
         part = jnp.dot(iq_t, e_ref[...], preferred_element_type=f32).T.reshape(SETB, 2, BLK // 2, 128)
         for q in range(2):
             ug_ref[q, h] = part[:, q].reshape(SETT // 2, 128)
-        keys = ik_ref[pl.ds(pl.multiple_of(h * SETT, SETT), SETT), :]
         for b in range(4):
             rows = slice(b * 256, (b + 1) * 256)
-            iqg_acc[rows, :] = iqg_acc[rows, :] + jnp.dot(e_ref[rows, :], keys, preferred_element_type=f32)
+            iqg_acc[rows, :] = iqg_acc[rows, :] + jnp.dot(e_ref[rows, :], ik_ref[h], preferred_element_type=f32)
 
     edges(0, ea_ref)
 
@@ -576,48 +609,30 @@
             iqg_ref[g, :, k * 128 : (k + 1) * 128] = iqg_acc[j * QROWS : (j + 1) * QROWS, :]
 
 
-def core(tab, kt, ik, mq, iq, w, sel_t, lengths, cot):
+def back(grad, iqr, row, ik):
     f32, bf = jnp.float32, jnp.bfloat16
     vm_spec = pl.BlockSpec(memory_space=VM)
     rows = IHEADS * QROWS
     return pl.pallas_call(
-        core_kernel,
-        name="core",
+        back_kernel,
+        name="back",
         out_shape=(
             jax.ShapeDtypeStruct((2, NH, SETT // 2, 128), f32),
             jax.ShapeDtypeStruct((NH, QROWS, 1024), f32),
             jax.ShapeDtypeStruct((NH, 8, 128), f32),
         ),
-        in_specs=[pl.BlockSpec(memory_space=pltpu.SMEM), pl.BlockSpec(memory_space=ANY), pl.BlockSpec(memory_space=ANY)]
-        + [vm_spec] * 6,
+        in_specs=[vm_spec] * 4,
         out_specs=(vm_spec,) * 3,
         scratch_shapes=[
-            VM((AUG, UNION), bf),
-            VM((UNION, 128), bf),
-            VM((256, UNION), f32),
-            VM((256, UNION), f32),
-            VM((256, 128), f32),
-            VM((256, 128), f32),
-            VM((256, AUG), bf),
-            VM((rows, UNION), f32),
             VM((rows, SETT), bf),
             VM((rows, SETT), bf),
-            VM((QROWS, UNION), f32),
-            VM((QROWS, UNION), f32),
-            VM((QROWS, UNION), f32),
-            VM((QROWS, UNION), f32),
             VM((128, 128), f32),
-            VM((128, 128), f32),
-            VM((32, QROWS, 128), f32),
             VM((IHEADS, QROWS, 128), f32),
-            VM((rows, 128), bf),
             VM((IHEADS, QROWS, 128), f32),
             VM((rows, 128), f32),
-            DMA((NH,)),
-            DMA((NH,)),
         ],
         compiler_params=pltpu.CompilerParams(vmem_limit_bytes=60 << 20),
-    )(tab, kt, ik, mq, iq, w, sel_t, lengths, cot)
+    )(grad, iqr, row, ik)
 
 
 HB = BLK // 2
@@ -692,12 +707,16 @@
             own[at : at + HB, :] = brecv[q, r].astype(own.dtype)
 
     rows = NC * HB
+
+    def kg_of(h, start, count):
+        return kg_out.at[h, pl.ds(start, count)]
+
     send_sums(0)
     take_sums(0)
     send_sums(1)
     send_blocks(0)
     take_blocks(0)
-    ga = gather_sets([(own, kg_out, 0, rows)], me_h, me_c, g_send, g_recv, loc_a)
+    ga = gather_sets([(own, kg_of, 0, rows)], me_h, me_c, g_send, g_recv, loc_a)
     next(ga)
     take_sums(1)
     send_blocks(1)
@@ -711,7 +730,7 @@
         sends.append(s)
     next(ga)
     take_blocks(1)
-    gb = gather_sets([(own, kg_out, rows, rows)], me_h, me_c, h_send, h_recv, loc_b)
+    gb = gather_sets([(own, kg_of, rows, rows)], me_h, me_c, h_send, h_recv, loc_b)
     next(gb)
     finish(ga, gb)
     for o in range(1, NH):
@@ -794,10 +813,11 @@
 def shards(main_query, latent, index_query, index_key, index_weight, selected, lengths, cotangent):
     sel_t = selected.T
     req, tab = make_plan(sel_t)
-    kt, ik, mq, iq, w, asked = fetch(
-        tab, req, latent.T, index_key.reshape(-1, BLK, WIDTH), main_query, index_query, index_weight.T
+    grad, iqr, row, asked, ik = forward(
+        tab, req, sel_t, lengths[None, :], cotangent[None, :],
+        latent.T, index_key.reshape(-1, BLK, WIDTH), main_query, index_query, index_weight.T,
     )
-    ug, iqg, wg = core(tab, kt, ik, mq, iq, w, sel_t, lengths[None, :], cotangent[None, :])
+    ug, iqg, wg = back(grad, iqr, row, ik)
     query_grad, weight_grad, kg = give_back(tab, ug, iqg, wg)
     key_grad = scatter(asked, kg, latent.shape[0])
     return query_grad, weight_grad.T, key_grad

time: 220 us -> 218 us (level)
  Pallas kernels: 218 us -> 215 us
    pallas_call x1, Pallas kernels: 74 us -> 70.9 us  [give_back(): pl.pallas_call(return_kernel, name='give_back', out_shape=(jax.ShapeDtype...]
where the time goes in v3:
time: 218 us; the launch traced here: 217 us
  Pallas kernels  215 us (99%)
    pallas_call x1, Pallas kernels, forward(): pl.pallas_call(forward_kernel, name='forward', out_shape=(jax.ShapeDtypeS...  126 us
    pallas_call x1, Pallas kernels, give_back(): pl.pallas_call(return_kernel, name='give_back', out_shape=(jax.ShapeDtype...  70.9 us
    pallas_call x1, Pallas kernels, back(): pl.pallas_call(back_kernel, name='back', out_shape=(jax.ShapeDtypeStruct(...  10.3 us
    pallas_call x1, Pallas kernels, scatter(): pl.pallas_call(scatter_kernel, name='scatter', out_shape=jax.ShapeDtypeSt...  5.35 us

profile of v3, /device:TPU:0, one launch (start us, length us, event | category | flops | bytes accessed | tf_op | source)
XLA Modules:
  0.0 217.3 jit_solution(12699220698305625365)
XLA Ops:
  0.6 2.2 plan.1
  2.8 126.5 %forward.1 = (f32[16,4096]{1,0:T(8,128)}, bf16[1024,128]{1,0:T(8,128)(2,1)}, f32[16,128]{1,0:T(8,128)}, s32[16,128]{1,0:T(8,128)}, bf16[8,512,128]{2,1,0:T(8,128)(2,1)}) custom-call(s32[16,128]{1,0:T(8,128)} %get-tuple-element.16.tab_s, s32[16,8,128]{2,1,0:T(8,128)} %get-tuple-element.17.req, s32[32,128]{1,0:T(8,128)} %bitcast.10, s32[1,128]{1,0:T(1,128)} %bitcast.13, ...), custom_call_target="tpu_custom_call" | custom-call | tf_op jit(solution)/shard_map/forward/pallas_call | solution.py:499
  129.3 10.3 %back.1 = (f32[2,8,256,128]{3,2,1,0:T(8,128)}, f32[8,16,1024]{2,1,0:T(8,128)}, f32[8,8,128]{2,1,0:T(8,128)}) custom-call(f32[16,4096]{1,0:T(8,128)} %get-tuple-element.18.grad_ref, bf16[1024,128]{1,0:T(8,128)(2,1)} %get-tuple-element.19.iqr_ref, f32[16,128]{1,0:T(8,128)} %get-tuple-element.20.row_ref, bf16[8,512,128]{2,1,0:T(8,128)(2,1)} %get-tuple-element.21.ik_ref), custom_call_target="tpu_custom_call" | custom-call | tf_op jit(solution)/shard_map/back/pallas_call | solution.py:616
  139.6 70.9 %give_back.1 = (f32[128,1024]{1,0:T(8,128)}, f32[8,128]{1,0:T(8,128)}, bf16[8,1024,128]{2,1,0:T(8,128)(2,1)}) custom-call(s32[16,128]{1,0:T(8,128)} %get-tuple-element.16.tab_s, f32[2,8,256,128]{3,2,1,0:T(8,128)} %get-tuple-element.22.ug_hbm, f32[8,16,1024]{2,1,0:T(8,128)} %get-tuple-element.23.iqg_hbm, f32[8,8,128]{2,1,0:T(8,128)} %get-tuple-element.24.wg_hbm), custom_call_target="tpu_custom_call" | custom-call | tf_op jit(solution)/shard_map/give_back/pallas_call | solution.py:759
  210.5 0.0 copy-start
  210.5 0.0 copy-start.1
  210.5 5.4 %scatter.1 = f32[8192,128]{1,0:T(8,128)} custom-call(s32[16,128]{1,0:T(8,128)} %get-tuple-element.27.asked_s, bf16[8,1024,128]{2,1,0:T(8,128)(2,1)} %get-tuple-element.28.kg_ref), custom_call_target="tpu_custom_call" | custom-call | tf_op jit(solution)/shard_map/scatter/pallas_call | solution.py:803
  215.9 0.0 copy-done
  215.9 0.8 copy.13
  216.7 0.0 copy-done.1
  216.7 0.6 copy.14
Async XLA Ops:
  210.5 5.4 %copy-start = (f32[128,1024]{1,0:T(8,128)S(1)}, f32[128,1024]{1,0:T(8,128)}, u32[]{:S(2)}) copy-start(f32[128,1024]{1,0:T(8,128)} %get-tuple-element.32) | copy-start | bytes 1572868
  210.5 6.2 %copy-start.1 = (f32[8,128]{1,0:T(8,128)S(1)}, f32[8,128]{1,0:T(8,128)}, u32[]{:S(2)}) copy-start(f32[8,128]{1,0:T(8,128)} %get-tuple-element.26) | copy-start | bytes 12292

commit v4 on v3

--- a/solution.py
+++ b/solution.py
@@ -248,13 +248,21 @@
         s.start()
         sends.append(s)
 
-    def query_copy(o, back=False):
-        h = lax.rem(me_h + (NH - o if back else o), NH)
+    def peer_of(n, back=False):
+        k = lax.rem(n, 4)
+        dx = k + lax.div(k, 2) * (5 - 2 * k)
+        dy = lax.div(n, 4)
+        x = lax.div(me_h, 2) + (4 - dx if back else dx)
+        y = lax.rem(me_h, 2) + dy
+        return 2 * lax.rem(x, 4) + lax.rem(y, 2)
+
+    def query_copy(n, back=False):
+        h = peer_of(jnp.int32(n), back)
         rows = pl.ds(0, QROWS) if back else pl.ds(pl.multiple_of(h * QROWS, QROWS), QROWS)
-        return remote(mq_hbm.at[rows], mq_ref.at[h if back else me_h], q_send.at[o], q_recv.at[o], (h, me_c))
-
-    def send_queries(o):
-        s = query_copy(o)
+        return remote(mq_hbm.at[rows], mq_ref.at[h if back else me_h], q_send.at[n], q_recv.at[n], (h, me_c))
+
+    def send_queries(n):
+        s = query_copy(n)
         s.start()
         sends.append(s)
 
@@ -265,8 +273,8 @@
             s = remote(src, dst.at[me_h], ss.at[o], rs.at[o], (h, me_c))
             s.start()
             sends.append(s)
-    for o in (2, 6, 4):
-        send_queries(o)
+    for n in (1, 2, 3):
+        send_queries(n)
     own_req.wait()
     for o in range(1, NC):
         c = lax.rem(me_c + NC - o, NC)
@@ -392,10 +400,9 @@
     next(gb)
     next(ga)
     next(gb)
+    send_queries(4)
     next(ga)
     next(gb)
-    for o in (1, 7, 3, 5):
-        send_queries(o)
     finish(ga)
 
     def index_chunk(i, carry):
@@ -414,6 +421,8 @@
 
     lax.fori_loop(0, NH // 2, index_chunk, 0)
     next(gb)
+    for n in (5, 6, 7):
+        send_queries(n)
     lax.fori_loop(NH // 2, NH, index_chunk, 0)
     keys_out = pltpu.make_async_copy(ik_ref, ik_out, loc.at[5])
     keys_out.start()
@@ -428,9 +437,8 @@
             qt_ref[k * QROWS : (k + 1) * QROWS, 0:LAT] = mq_ref[g, :, k * LAT : (k + 1) * LAT]
 
     def arrive(n):
-        o = lax.rem(2 * n, NH) + lax.div(n, NH // 2)
-        query_copy(o, True).wait_recv()
-        load_queries(lax.rem(me_h + NH - o, NH))
+        query_copy(n, True).wait_recv()
+        load_queries(peer_of(jnp.int32(n), True))
 
     def score_tile(t, s_ref, m_ref):
         cols = slice(t * TILE, (t + 1) * TILE)
@@ -545,25 +553,35 @@
     )(tab, req, sel_t, lengths, cot, lat_t, index_key, main_query, index_query, weight_t)
 
 
-def back_kernel(
-    grad_ref, iqr_ref, row_ref, ik_ref,
-    ug_ref, iqg_ref, wg_ref,
-    ea_ref, eb_ref, wq_ref, wb_ref, wcol_ref, iqg_acc,
+HB = BLK // 2
+
+
+def return_kernel(
+    tab_s, grad_ref, iqr_ref, row_ref, ik_ref,
+    iqg_out, wg_out, kg_out,
+    ea_ref, eb_ref, wq_ref, wb_ref, wcol_ref, iqg_acc, iqt_ref, iqg, wg, ug,
+    urecv, sums, slots, brecv, own, wrecv,
+    u_send, u_recv, i_send, i_recv, w_send, w_recv, b_send, b_recv, g_send, g_recv, h_send, h_recv, loc, loc_a, loc_b,
 ):
-    me = lax.axis_index("head")
-    mine = pl.ds(pl.multiple_of(me * QROWS, QROWS), QROWS)
     f32, bf = jnp.float32, jnp.bfloat16
+    me_h = lax.axis_index("head")
+    me_c = lax.axis_index("ctx")
+    my_q = pl.ds(pl.multiple_of(me_h * QROWS, QROWS), QROWS)
+    start_barrier(me_h, me_c)
     lane = iota((QROWS, 128), 1)
     row = row_ref[...]
     for j in range(IHEADS):
         wb_ref[j] = jnp.broadcast_to(row[:, 64 + j : 65 + j], (QROWS, 128))
     wcol_ref[...] = jnp.zeros(wcol_ref.shape, f32)
     iqg_acc[...] = jnp.zeros(iqg_acc.shape, f32)
-    iq_t = iqr_ref[...].T
-
-    def edges(h, e_ref):
-        cols = pl.ds(pl.multiple_of(h * SETT, SETT), SETT)
-        grad = grad_ref[:, cols]
+    iqt_ref[...] = iqr_ref[...].T
+
+    def whose(n):
+        return lax.rem(me_h + 1 + n, NH)
+
+    def edges(n, e_ref):
+        h = whose(n)
+        grad = grad_ref[:, pl.ds(pl.multiple_of(h * SETT, SETT), SETT)]
         for b in range(4):
             pre_b = lax.dot_general(
                 iqr_ref[b * 256 : (b + 1) * 256, :], ik_ref[h], (((1,), (1,)), ((), ())), preferred_element_type=f32
@@ -576,111 +594,66 @@
                 wcol_ref[j] = wcol_ref[j] + sum(part[:, t * 128 : (t + 1) * 128] for t in range(SETT // 128))
                 e_ref[j * QROWS : (j + 1) * QROWS, :] = jnp.where(pre > 0.0, grad * w, 0.0).astype(bf)
 
-    def products(h, e_ref):
-        part = jnp.dot(iq_t, e_ref[...], preferred_element_type=f32).T.reshape(SETB, 2, BLK // 2, 128)
+    def products(n, e_ref):
+        h = whose(n)
+        part = jnp.dot(iqt_ref[...], e_ref[...], preferred_element_type=f32).T.reshape(SETB, 2, HB, 128)
         for q in range(2):
-            ug_ref[q, h] = part[:, q].reshape(SETT // 2, 128)
+            ug[q, n] = part[:, q].reshape(SETT // 2, 128)
         for b in range(4):
             rows = slice(b * 256, (b + 1) * 256)
             iqg_acc[rows, :] = iqg_acc[rows, :] + jnp.dot(e_ref[rows, :], ik_ref[h], preferred_element_type=f32)
 
+    def sum_copy(q, n):
+        return remote(
+            ug.at[q, n], urecv.at[q, n], u_send.at[q * NH + n], u_recv.at[q * NH + n], (whose(n), me_c)
+        )
+
     edges(0, ea_ref)
 
     def two_sets(i, carry):
         edges(2 * i + 1, eb_ref)
         products(2 * i, ea_ref)
+        sum_copy(0, 2 * i).start()
         edges(2 * i + 2, ea_ref)
         products(2 * i + 1, eb_ref)
+        sum_copy(0, 2 * i + 1).start()
         return carry
 
     lax.fori_loop(0, NH // 2 - 1, two_sets, 0)
     edges(NH - 1, eb_ref)
     products(NH - 2, ea_ref)
+    sum_copy(0, NH - 2).start()
+    for n in range(NH - 1):
+        sum_copy(1, n).start()
     products(NH - 1, eb_ref)
     wrow = jnp.zeros((QROWS, 128), f32)
     for j in range(IHEADS):
         wrow = jnp.where(lane == j, jnp.sum(wcol_ref[j], axis=1, keepdims=True), wrow)
     wq_ref[...] = jnp.zeros((128, 128), f32)
-    wq_ref[mine, :] = wrow
-    wg_ref[...] = wq_ref[...].T[0:IHEADS, :].reshape(NH, 8, 128)
+    wq_ref[my_q, :] = wrow
+    wg[...] = wq_ref[...].T[0:IHEADS, :].reshape(NH, 8, 128)
     for g in range(NH):
         for k in range(8):
             j = g * 8 + k
-            iqg_ref[g, :, k * 128 : (k + 1) * 128] = iqg_acc[j * QROWS : (j + 1) * QROWS, :]
-
-
-def back(grad, iqr, row, ik):
-    f32, bf = jnp.float32, jnp.bfloat16
-    vm_spec = pl.BlockSpec(memory_space=VM)
-    rows = IHEADS * QROWS
-    return pl.pallas_call(
-        back_kernel,
-        name="back",
-        out_shape=(
-            jax.ShapeDtypeStruct((2, NH, SETT // 2, 128), f32),
-            jax.ShapeDtypeStruct((NH, QROWS, 1024), f32),
-            jax.ShapeDtypeStruct((NH, 8, 128), f32),
-        ),
-        in_specs=[vm_spec] * 4,
-        out_specs=(vm_spec,) * 3,
-        scratch_shapes=[
-            VM((rows, SETT), bf),
-            VM((rows, SETT), bf),
-            VM((128, 128), f32),
-            VM((IHEADS, QROWS, 128), f32),
-            VM((IHEADS, QROWS, 128), f32),
-            VM((rows, 128), f32),
-        ],
-        compiler_params=pltpu.CompilerParams(vmem_limit_bytes=60 << 20),
-    )(grad, iqr, row, ik)
-
-
-HB = BLK // 2
-
-
-def return_kernel(
-    tab_s, ug_hbm, iqg_hbm, wg_hbm,
-    iqg_out, wg_out, kg_out,
-    urecv, sums, slots, brecv, own, wrecv,
-    u_send, u_recv, i_send, i_recv, w_send, w_recv, b_send, b_recv, g_send, g_recv, h_send, h_recv, loc, loc_a, loc_b,
-):
-    me_h = lax.axis_index("head")
-    me_c = lax.axis_index("ctx")
-    my_q = pl.ds(pl.multiple_of(me_h * QROWS, QROWS), QROWS)
+            iqg[g, :, k * 128 : (k + 1) * 128] = iqg_acc[j * QROWS : (j + 1) * QROWS, :]
     own_copies = [
-        pltpu.make_async_copy(ug_hbm.at[0, me_h], urecv.at[0, me_h], loc.at[0]),
-        pltpu.make_async_copy(ug_hbm.at[1, me_h], urecv.at[1, me_h], loc.at[1]),
-        pltpu.make_async_copy(iqg_hbm.at[me_h], iqg_out.at[my_q], loc.at[2]),
-        pltpu.make_async_copy(wg_hbm.at[me_h], wrecv.at[me_h], loc.at[3]),
+        pltpu.make_async_copy(iqg.at[me_h], iqg_out.at[my_q], loc.at[2]),
+        pltpu.make_async_copy(wg.at[me_h], wrecv.at[me_h], loc.at[3]),
     ]
     for c in own_copies:
         c.start()
-    start_barrier(me_h, me_c)
-    sends = []
-
-    def send_sums(q):
-        for o in (1, 7, 3, 5, 2, 6, 4):
-            h = lax.rem(me_h + o, NH)
-            s = remote(
-                ug_hbm.at[q, h], urecv.at[q, me_h], u_send.at[q * NH + o], u_recv.at[q * NH + o], (h, me_c)
-            )
-            s.start()
-            sends.append(s)
+    sends = [sum_copy(q, n) for q in range(2) for n in range(NH - 1)]
 
     def take_sums(q):
-        own_copies[q].wait()
-        for o in range(1, NH):
-            h = lax.rem(me_h + NH - o, NH)
-            remote(
-                ug_hbm.at[q, h], urecv.at[q, h], u_send.at[q * NH + o], u_recv.at[q * NH + o], (h, me_c)
-            ).wait_recv()
+        for n in range(NH - 1):
+            sum_copy(q, n).wait_recv()
 
     def send_blocks(q):
         for j in range(SETB):
             rows = slice(j * HB, (j + 1) * HB)
-            acc = urecv[q, 0, rows, :]
-            for h in range(1, NH):
-                acc = acc + urecv[q, h, rows, :]
+            acc = ug[q, NH - 1, rows, :]
+            for n in range(NH - 1):
+                acc = acc + urecv[q, n, rows, :]
             sums[q, j] = acc
         sums[q, SETB] = jnp.zeros((HB, 128), jnp.float32)
         for o in range(1, NC + 1):
@@ -711,9 +684,7 @@
     def kg_of(h, start, count):
         return kg_out.at[h, pl.ds(start, count)]
 
-    send_sums(0)
     take_sums(0)
-    send_sums(1)
     send_blocks(0)
     take_blocks(0)
     ga = gather_sets([(own, kg_of, 0, rows)], me_h, me_c, g_send, g_recv, loc_a)
@@ -722,10 +693,10 @@
     send_blocks(1)
     for o in range(1, NH):
         h = lax.rem(me_h + o, NH)
-        s = remote(iqg_hbm.at[h], iqg_out.at[my_q], i_send.at[o], i_recv.at[o], (h, me_c))
+        s = remote(iqg.at[h], iqg_out.at[my_q], i_send.at[o], i_recv.at[o], (h, me_c))
         s.start()
         sends.append(s)
-        s = remote(wg_hbm.at[h], wrecv.at[me_h], w_send.at[o], w_recv.at[o], (h, me_c))
+        s = remote(wg.at[h], wrecv.at[me_h], w_send.at[o], w_recv.at[o], (h, me_c))
         s.start()
         sends.append(s)
     next(ga)
@@ -736,12 +707,12 @@
     for o in range(1, NH):
         h = lax.rem(me_h + NH - o, NH)
         remote(
-            iqg_hbm.at[h], iqg_out.at[pl.ds(pl.multiple_of(h * QROWS, QROWS), QROWS)],
+            iqg.at[h], iqg_out.at[pl.ds(pl.multiple_of(h * QROWS, QROWS), QROWS)],
             i_send.at[o], i_recv.at[o], (h, me_c),
         ).wait_recv()
-        remote(wg_hbm.at[h], wrecv.at[h], w_send.at[o], w_recv.at[o], (h, me_c)).wait_recv()
-    own_copies[2].wait()
-    own_copies[3].wait()
+        remote(wg.at[h], wrecv.at[h], w_send.at[o], w_recv.at[o], (h, me_c)).wait_recv()
+    for c in own_copies:
+        c.wait()
     acc = wrecv[0]
     for h in range(1, NH):
         acc = acc + wrecv[h]
@@ -753,9 +724,11 @@
 SENT = jnp.bfloat16
 
 
-def give_back(tab, ug, iqg, wg):
-    f32 = jnp.float32
+def give_back(tab, grad, iqr, row, ik):
+    f32, bf = jnp.float32, jnp.bfloat16
     any_spec = pl.BlockSpec(memory_space=ANY)
+    vm_spec = pl.BlockSpec(memory_space=VM)
+    rows = IHEADS * QROWS
     return pl.pallas_call(
         return_kernel,
         name="give_back",
@@ -764,10 +737,20 @@
             jax.ShapeDtypeStruct((8, 128), f32),
             jax.ShapeDtypeStruct((NH, NC * BLK, 128), SENT),
         ),
-        in_specs=[pl.BlockSpec(memory_space=pltpu.SMEM)] + [any_spec] * 3,
-        out_specs=(any_spec, pl.BlockSpec(memory_space=VM), any_spec),
+        in_specs=[pl.BlockSpec(memory_space=pltpu.SMEM)] + [vm_spec] * 4,
+        out_specs=(any_spec, vm_spec, any_spec),
         scratch_shapes=[
+            VM((rows, SETT), bf),
+            VM((rows, SETT), bf),
+            VM((128, 128), f32),
+            VM((IHEADS, QROWS, 128), f32),
+            VM((IHEADS, QROWS, 128), f32),
+            VM((rows, 128), f32),
+            VM((128, rows), bf),
+            VM((NH, QROWS, 1024), f32),
+            VM((NH, 8, 128), f32),
             VM((2, NH, SETT // 2, 128), f32),
+            VM((2, NH - 1, SETT // 2, 128), f32),
             VM((2, SETB + 1, HB, 128), f32),
             VM((2, NC, HB, 128), f32),
             VM((2, NC, HB, 128), f32),
@@ -780,7 +763,7 @@
         compiler_params=pltpu.CompilerParams(
             collective_id=1, has_side_effects=True, vmem_limit_bytes=60 << 20
         ),
-    )(tab, ug, iqg, wg)
+    )(tab, grad, iqr, row, ik)
 
 
 def scatter_kernel(asked_s, kg_ref, out_ref):
@@ -817,8 +800,7 @@
         tab, req, sel_t, lengths[None, :], cotangent[None, :],
         latent.T, index_key.reshape(-1, BLK, WIDTH), main_query, index_query, index_weight.T,
     )
-    ug, iqg, wg = back(grad, iqr, row, ik)
-    query_grad, weight_grad, kg = give_back(tab, ug, iqg, wg)
+    query_grad, weight_grad, kg = give_back(tab, grad, iqr, row, ik)
     key_grad = scatter(asked, kg, latent.shape[0])
     return query_grad, weight_grad.T, key_grad
 

time: 218 us -> 194 us (0.89)
  Pallas kernels: 215 us -> 192 us
    pallas_call x1, Pallas kernels: 126 us -> 112 us  [forward(): pl.pallas_call(forward_kernel, name='forward', out_shape=(jax.ShapeDtypeS...]
    pallas_call x1 -> x0, Pallas kernels: 10.3 us -> none  [back(): pl.pallas_call(back_kernel, name='back', out_shape=(jax.ShapeDtypeStruct(...]
where the time goes in v4:
time: 194 us
  Pallas kernels  192 us (99%)
    pallas_call x1, Pallas kernels, forward(): pl.pallas_call(forward_kernel, name='forward', out_shape=(jax.ShapeDtypeS...  112 us
    pallas_call x1, Pallas kernels, give_back(): pl.pallas_call(return_kernel, name='give_back', out_shape=(jax.ShapeDtype...  72.7 us
    pallas_call x1, Pallas kernels, scatter(): pl.pallas_call(scatter_kernel, name='scatter', out_shape=jax.ShapeDtypeSt...  5.35 us

profile of v4, /device:TPU:0, one launch (start us, length us, event | category | flops | bytes accessed | tf_op | source)
XLA Modules:
  0.0 194.0 jit_solution(14365271445059622696)
XLA Ops:
  0.6 2.2 %plan.1 = (s32[16,8,128]{2,1,0:T(8,128)}, s32[16,128]{1,0:T(8,128)}) custom-call(s32[32,128]{1,0:T(8,128)} %bitcast.9), custom_call_target="tpu_custom_call" | custom-call | tf_op jit(solution)/shard_map/plan/pallas_call | solution.py:197
  2.8 111.8 %forward.1 = (f32[16,4096]{1,0:T(8,128)}, bf16[1024,128]{1,0:T(8,128)(2,1)}, f32[16,128]{1,0:T(8,128)}, s32[16,128]{1,0:T(8,128)}, bf16[8,512,128]{2,1,0:T(8,128)(2,1)}) custom-call(s32[16,128]{1,0:T(8,128)} %get-tuple-element.13.tab_s, s32[16,8,128]{2,1,0:T(8,128)} %get-tuple-element.14.req, s32[32,128]{1,0:T(8,128)} %bitcast.10, s32[1,128]{1,0:T(1,128)} %bitcast.13, ...), custom_call_target="tpu_custom_call" | custom-call | tf_op jit(solution)/shard_map/forward/pallas_call | solution.py:507
  114.6 72.7 %give_back.1 = (f32[128,1024]{1,0:T(8,128)}, f32[8,128]{1,0:T(8,128)}, bf16[8,1024,128]{2,1,0:T(8,128)(2,1)}) custom-call(s32[16,128]{1,0:T(8,128)} %get-tuple-element.13.tab_s, f32[16,4096]{1,0:T(8,128)} %get-tuple-element.15.grad_ref, bf16[1024,128]{1,0:T(8,128)(2,1)} %get-tuple-element.16.iqr_ref, f32[16,128]{1,0:T(8,128)} %get-tuple-element.17.row_ref, ...), custom_call_target="tpu_custom_call" | custom-call | tf_op jit(solution)/shard_map/give_back/pallas_call | solution.py:732
  187.3 0.0 copy-start
  187.3 0.0 copy-start.1
  187.3 5.4 %scatter.1 = f32[8192,128]{1,0:T(8,128)} custom-call(s32[16,128]{1,0:T(8,128)} %get-tuple-element.21.asked_s, bf16[8,1024,128]{2,1,0:T(8,128)(2,1)} %get-tuple-element.22.kg_ref), custom_call_target="tpu_custom_call" | custom-call | tf_op jit(solution)/shard_map/scatter/pallas_call | solution.py:786
  192.6 0.0 copy-done
  192.6 0.8 copy.13
  193.4 0.0 copy-done.1
  193.4 0.6 copy.14
Async XLA Ops:
  187.3 5.4 %copy-start = (f32[128,1024]{1,0:T(8,128)S(1)}, f32[128,1024]{1,0:T(8,128)}, u32[]{:S(2)}) copy-start(f32[128,1024]{1,0:T(8,128)} %get-tuple-element.26) | copy-start | bytes 1572868
  187.3 6.2 %copy-start.1 = (f32[8,128]{1,0:T(8,128)S(1)}, f32[8,128]{1,0:T(8,128)}, u32[]{:S(2)}) copy-start(f32[8,128]{1,0:T(8,128)} %get-tuple-element.20) | copy-start | bytes 12292

commit v5 on v4

--- a/solution.py
+++ b/solution.py
@@ -104,6 +104,8 @@
     go(1, me_h, 0, right, True)
     go(2, me_h, 0, left, True)
     yield
+    for c in locals_:
+        c.wait()
     wait(0, flip, 0, partner)
     go(3, flip, 0, right)
     go(4, flip, 0, left)
@@ -122,8 +124,6 @@
     wait(6, far, 2, left)
     wait(7, flipped(far), 1, right)
     wait(8, flipped(far), 2, left)
-    for c in locals_:
-        c.wait()
     for c in sent:
         c.wait_send()
 
@@ -217,10 +217,10 @@
     tab_s, req, sel_ref, len_ref, cot_ref, lat_hbm, ik_hbm, mq_hbm, iq_hbm, w_hbm,
     grad_ref, iqr_ref, wrow_ref, asked_out, ik_out,
     lat_v, ik_v, stage, recv_a, recv_b, own, own_ik, asked, asked_s,
-    kt_ref, ik_ref, mq_ref, iq_ref, w_ref,
+    kt_ref, ik_ref, mq_ref, iq_ref, w_ref, passing,
     sa_ref, sb_ref, ma_ref, mb_ref, qt_ref, bias_ref, tgt_ref, idx_ref, meta_ref, selb_ref, wb_ref,
     q_send, q_recv, i_send, i_recv, w_send, w_recv, r_send, r_recv, b_send, b_recv, c_send, c_recv,
-    g_send, g_recv, h_send, h_recv, loc, loc_a, loc_b, l_sem,
+    g_send, g_recv, h_send, h_recv, loc, loc_a, loc_b, l_sem, p_send, p_recv,
 ):
     f32, bf = jnp.float32, jnp.bfloat16
     me_h = lax.axis_index("head")
@@ -263,6 +263,26 @@
 
     def send_queries(n):
         s = query_copy(n)
+        s.start()
+        sends.append(s)
+
+    partner = me_h + 1 - 2 * lax.rem(me_h, 2)
+
+    def relay_copy(n, back=False):
+        h = peer_of(jnp.int32(n))
+        rows = pl.ds(0, QROWS) if back else pl.ds(pl.multiple_of(h * QROWS, QROWS), QROWS)
+        return remote(mq_hbm.at[rows], passing.at[n - 5], p_send.at[n - 5], p_recv.at[n - 5], (partner, me_c))
+
+    def send_over(n):
+        s = relay_copy(n)
+        s.start()
+        sends.append(s)
+
+    def pass_on(n):
+        relay_copy(n, True).wait_recv()
+        dx = (1, 3, 2)[n - 5]
+        to = lax.rem(me_h + 2 * dx, NH)
+        s = remote(passing.at[n - 5], mq_ref.at[partner], q_send.at[n], q_recv.at[n], (to, me_c))
         s.start()
         sends.append(s)
 
@@ -397,15 +417,7 @@
         [(own, kt_of, FIRST, HALF - FIRST), (own, kt_of, HALF + FIRST, HALF - FIRST)],
         me_h, me_c, h_send, h_recv, loc_b,
     )
-    next(gb)
-    next(ga)
-    next(gb)
-    send_queries(4)
-    next(ga)
-    next(gb)
-    finish(ga)
-
-    def index_chunk(i, carry):
+    def index_scores(i):
         cols = pl.ds(pl.multiple_of(i * SETT, SETT), SETT)
         acc = jnp.zeros((QROWS, SETT), f32)
         for b in range(4):
@@ -417,13 +429,33 @@
                 w = jnp.concatenate([wb_ref[b * 16 + j]] * (SETT // 128), axis=1)
                 acc = acc + w * jnp.maximum(pre[j * QROWS : (j + 1) * QROWS, :], 0.0)
         idx_ref[:, cols] = acc + bias_ref[:, cols]
-        return carry
-
-    lax.fori_loop(0, NH // 2, index_chunk, 0)
+
+    flip = partner
+    near_l, near_r, far = (lax.rem(me_h + o, NH) for o in (6, 2, 4))
+
+    def other(h):
+        return h + 1 - 2 * lax.rem(h, 2)
+
+    next(gb)
+    next(ga)
+    next(gb)
+    send_queries(4)
+    for n in (5, 6, 7):
+        send_over(n)
+    index_scores(me_h)
+    index_scores(flip)
+    next(ga)
+    next(gb)
+    index_scores(near_l)
+    index_scores(near_r)
     next(gb)
     for n in (5, 6, 7):
-        send_queries(n)
-    lax.fori_loop(NH // 2, NH, index_chunk, 0)
+        pass_on(n)
+    index_scores(other(near_l))
+    index_scores(other(near_r))
+    finish(ga)
+    index_scores(far)
+    index_scores(other(far))
     keys_out = pltpu.make_async_copy(ik_ref, ik_out, loc.at[5])
     keys_out.start()
     v = idx_ref[...]
@@ -531,6 +563,7 @@
             VM((NH, QROWS, main_query.shape[1]), bf),
             VM((NH, QROWS, index_query.shape[1]), bf),
             VM((NH, 8, 128), f32),
+            VM((3, QROWS, main_query.shape[1]), bf),
             VM((256, UNION), f32),
             VM((256, UNION), f32),
             VM((256, 128), f32),
@@ -545,7 +578,7 @@
             DMA((NH,)), DMA((NH,)), DMA((NH,)), DMA((NH,)), DMA((NH,)), DMA((NH,)),
             DMA((NC,)), DMA((NC,)), DMA((NC,)), DMA((NC,)), DMA((NC,)), DMA((NC,)),
             DMA((27,)), DMA((27,)), DMA((18,)), DMA((18,)), DMA((9,)), DMA((3,)), DMA((3,)),
-            DMA((lat_t.shape[1] // 128,)),
+            DMA((lat_t.shape[1] // 128,)), DMA((3,)), DMA((3,)),
         ],
         compiler_params=pltpu.CompilerParams(
             collective_id=0, has_side_effects=True, vmem_limit_bytes=60 << 20
@@ -779,7 +812,7 @@
             out_ref[rows, :] = out_ref[rows, :] + part.astype(jnp.float32)
         return carry
 
-    lax.fori_loop(0, NH * NC, one, 0)
+    lax.fori_loop(0, NH * NC, one, 0, unroll=4)
 
 
 def scatter(asked, kg, tokens):

time: 194 us -> 187 us (0.964)
  Pallas kernels: 192 us -> 184 us
    pallas_call x1, Pallas kernels: 72.7 us -> 67.8 us  [give_back(): pl.pallas_call(return_kernel, name='give_back', out_shape=(jax.ShapeDtype...]
    pallas_call x1, Pallas kernels: 112 us -> 109 us  [forward(): pl.pallas_call(forward_kernel, name='forward', out_shape=(jax.ShapeDtypeS...]
where the time goes in v5:
time: 187 us; the launch traced here: 186 us
  Pallas kernels  184 us (98%)
    pallas_call x1, Pallas kernels, forward(): pl.pallas_call(forward_kernel, name='forward', out_shape=(jax.ShapeDtypeS...  109 us
    pallas_call x1, Pallas kernels, give_back(): pl.pallas_call(return_kernel, name='give_back', out_shape=(jax.ShapeDtype...  67.8 us
    pallas_call x1, Pallas kernels, scatter(): pl.pallas_call(scatter_kernel, name='scatter', out_shape=jax.ShapeDtypeSt...  4.85 us

profile of v5, /device:TPU:0, one launch (start us, length us, event | category | flops | bytes accessed | tf_op | source)
XLA Modules:
  0.0 185.7 jit_solution(6519031907268661230)
XLA Ops:
  0.6 2.2 %plan.1 = (s32[16,8,128]{2,1,0:T(8,128)}, s32[16,128]{1,0:T(8,128)}) custom-call(s32[32,128]{1,0:T(8,128)} %bitcast.9), custom_call_target="tpu_custom_call" | custom-call | tf_op jit(solution)/shard_map/plan/pallas_call | solution.py:197
  2.8 108.9 %forward.1 = (f32[16,4096]{1,0:T(8,128)}, bf16[1024,128]{1,0:T(8,128)(2,1)}, f32[16,128]{1,0:T(8,128)}, s32[16,128]{1,0:T(8,128)}, bf16[8,512,128]{2,1,0:T(8,128)(2,1)}) custom-call(s32[16,128]{1,0:T(8,128)} %get-tuple-element.13.tab_s, s32[16,8,128]{2,1,0:T(8,128)} %get-tuple-element.14.req, s32[32,128]{1,0:T(8,128)} %bitcast.10, s32[1,128]{1,0:T(1,128)} %bitcast.13, ...), custom_call_target="tpu_custom_call" | custom-call | tf_op jit(solution)/shard_map/forward/pallas_call | solution.py:539
  111.7 67.8 %give_back.1 = (f32[128,1024]{1,0:T(8,128)}, f32[8,128]{1,0:T(8,128)}, bf16[8,1024,128]{2,1,0:T(8,128)(2,1)}) custom-call(s32[16,128]{1,0:T(8,128)} %get-tuple-element.13.tab_s, f32[16,4096]{1,0:T(8,128)} %get-tuple-element.15.grad_ref, bf16[1024,128]{1,0:T(8,128)(2,1)} %get-tuple-element.16.iqr_ref, f32[16,128]{1,0:T(8,128)} %get-tuple-element.17.row_ref, ...), custom_call_target="tpu_custom_call" | custom-call | tf_op jit(solution)/shard_map/give_back/pallas_call | solution.py:765
  179.5 0.0 copy-start
  179.5 0.0 copy-start.1
  179.5 4.8 %scatter.1 = f32[8192,128]{1,0:T(8,128)} custom-call(s32[16,128]{1,0:T(8,128)} %get-tuple-element.21.asked_s, bf16[8,1024,128]{2,1,0:T(8,128)(2,1)} %get-tuple-element.22.kg_ref), custom_call_target="tpu_custom_call" | custom-call | tf_op jit(solution)/shard_map/scatter/pallas_call | solution.py:819
  184.3 0.0 copy-done
  184.3 0.8 copy.13
  185.1 0.0 copy-done.1
  185.1 0.6 copy.14
Async XLA Ops:
  179.5 4.9 %copy-start = (f32[128,1024]{1,0:T(8,128)S(1)}, f32[128,1024]{1,0:T(8,128)}, u32[]{:S(2)}) copy-start(f32[128,1024]{1,0:T(8,128)} %get-tuple-element.26) | copy-start | bytes 1572868
  179.5 5.7 %copy-start.1 = (f32[8,128]{1,0:T(8,128)S(1)}, f32[8,128]{1,0:T(8,128)}, u32[]{:S(2)}) copy-start(f32[8,128]{1,0:T(8,128)} %get-tuple-element.20) | copy-start | bytes 12292

commit v6 on v5

--- a/solution.py
+++ b/solution.py
@@ -609,11 +609,16 @@
     iqg_acc[...] = jnp.zeros(iqg_acc.shape, f32)
     iqt_ref[...] = iqr_ref[...].T
 
+    partner = me_h + 1 - 2 * lax.rem(me_h, 2)
+
     def whose(n):
-        return lax.rem(me_h + 1 + n, NH)
+        k = lax.rem(n + 1, 4)
+        x = lax.div(me_h, 2) + k + lax.div(k, 2) * (5 - 2 * k)
+        y = lax.rem(me_h, 2) + 1 - lax.div(n, 4)
+        return 2 * lax.rem(x, 4) + lax.rem(y, 2)
 
     def edges(n, e_ref):
-        h = whose(n)
+        h = whose(jnp.int32(n))
         grad = grad_ref[:, pl.ds(pl.multiple_of(h * SETT, SETT), SETT)]
         for b in range(4):
             pre_b = lax.dot_general(
@@ -628,7 +633,7 @@
                 e_ref[j * QROWS : (j + 1) * QROWS, :] = jnp.where(pre > 0.0, grad * w, 0.0).astype(bf)
 
     def products(n, e_ref):
-        h = whose(n)
+        h = whose(jnp.int32(n))
         part = jnp.dot(iqt_ref[...], e_ref[...], preferred_element_type=f32).T.reshape(SETB, 2, HB, 128)
         for q in range(2):
             ug[q, n] = part[:, q].reshape(SETT // 2, 128)
@@ -636,28 +641,29 @@
             rows = slice(b * 256, (b + 1) * 256)
             iqg_acc[rows, :] = iqg_acc[rows, :] + jnp.dot(e_ref[rows, :], ik_ref[h], preferred_element_type=f32)
 
-    def sum_copy(q, n):
-        return remote(
-            ug.at[q, n], urecv.at[q, n], u_send.at[q * NH + n], u_recv.at[q * NH + n], (whose(n), me_c)
-        )
+    def sum_copy(q, n, to):
+        return remote(ug.at[q, n], urecv.at[q, n], u_send.at[q * NH + n], u_recv.at[q * NH + n], (to, me_c))
 
     edges(0, ea_ref)
 
     def two_sets(i, carry):
         edges(2 * i + 1, eb_ref)
         products(2 * i, ea_ref)
-        sum_copy(0, 2 * i).start()
+        sum_copy(0, 2 * i, partner).start()
         edges(2 * i + 2, ea_ref)
         products(2 * i + 1, eb_ref)
-        sum_copy(0, 2 * i + 1).start()
+        sum_copy(0, 2 * i + 1, partner).start()
         return carry
 
-    lax.fori_loop(0, NH // 2 - 1, two_sets, 0)
-    edges(NH - 1, eb_ref)
-    products(NH - 2, ea_ref)
-    sum_copy(0, NH - 2).start()
-    for n in range(NH - 1):
-        sum_copy(1, n).start()
+    lax.fori_loop(0, 2, two_sets, 0)
+    for n in range(4):
+        sum_copy(1, n, partner).start()
+    edges(5, eb_ref)
+    products(4, ea_ref)
+    edges(6, ea_ref)
+    products(5, eb_ref)
+    edges(7, eb_ref)
+    products(6, ea_ref)
     products(NH - 1, eb_ref)
     wrow = jnp.zeros((QROWS, 128), f32)
     for j in range(IHEADS):
@@ -675,17 +681,26 @@
     ]
     for c in own_copies:
         c.start()
-    sends = [sum_copy(q, n) for q in range(2) for n in range(NH - 1)]
+    sends = [sum_copy(q, n, partner) for q in range(2) for n in range(4)]
+
+    def pass_sums(q):
+        for n in range(4, 7):
+            sum_copy(q, n - 4, partner).wait_recv()
+            ug[q, n] = ug[q, n] + urecv[q, n - 4]
+            s = sum_copy(q, n, whose(jnp.int32(n)))
+            s.start()
+            sends.append(s)
 
     def take_sums(q):
-        for n in range(NH - 1):
-            sum_copy(q, n).wait_recv()
+        sum_copy(q, 3, partner).wait_recv()
+        for n in range(4, 7):
+            sum_copy(q, n, partner).wait_recv()
 
     def send_blocks(q):
         for j in range(SETB):
             rows = slice(j * HB, (j + 1) * HB)
             acc = ug[q, NH - 1, rows, :]
-            for n in range(NH - 1):
+            for n in range(3, NH - 1):
                 acc = acc + urecv[q, n, rows, :]
             sums[q, j] = acc
         sums[q, SETB] = jnp.zeros((HB, 128), jnp.float32)
@@ -717,8 +732,10 @@
     def kg_of(h, start, count):
         return kg_out.at[h, pl.ds(start, count)]
 
+    pass_sums(0)
     take_sums(0)
     send_blocks(0)
+    pass_sums(1)
     take_blocks(0)
     ga = gather_sets([(own, kg_of, 0, rows)], me_h, me_c, g_send, g_recv, loc_a)
     next(ga)

time: 187 us -> 185 us (0.989)
  Pallas kernels: 184 us -> 182 us
where the time goes in v6:
time: 185 us; the launch traced here: 184 us
  Pallas kernels  182 us (98%)
    pallas_call x1, Pallas kernels, forward(): pl.pallas_call(forward_kernel, name='forward', out_shape=(jax.ShapeDtypeS...  109 us
    pallas_call x1, Pallas kernels, give_back(): pl.pallas_call(return_kernel, name='give_back', out_shape=(jax.ShapeDtype...  66 us
    pallas_call x1, Pallas kernels, scatter(): pl.pallas_call(scatter_kernel, name='scatter', out_shape=jax.ShapeDtypeSt...  4.85 us

profile of v6, /device:TPU:0, one launch (start us, length us, event | category | flops | bytes accessed | tf_op | source)
XLA Modules:
  0.0 184.0 jit_solution(8090159965643385941)
XLA Ops:
  0.6 2.2 %plan.1 = (s32[16,8,128]{2,1,0:T(8,128)}, s32[16,128]{1,0:T(8,128)}) custom-call(s32[32,128]{1,0:T(8,128)} %bitcast.9), custom_call_target="tpu_custom_call" | custom-call | tf_op jit(solution)/shard_map/plan/pallas_call | solution.py:197
  2.8 108.9 %forward.1 = (f32[16,4096]{1,0:T(8,128)}, bf16[1024,128]{1,0:T(8,128)(2,1)}, f32[16,128]{1,0:T(8,128)}, s32[16,128]{1,0:T(8,128)}, bf16[8,512,128]{2,1,0:T(8,128)(2,1)}) custom-call(s32[16,128]{1,0:T(8,128)} %get-tuple-element.13.tab_s, s32[16,8,128]{2,1,0:T(8,128)} %get-tuple-element.14.req, s32[32,128]{1,0:T(8,128)} %bitcast.10, s32[1,128]{1,0:T(1,128)} %bitcast.13, ...), custom_call_target="tpu_custom_call" | custom-call | tf_op jit(solution)/shard_map/forward/pallas_call | solution.py:539
  111.7 66.0 %give_back.1 = (f32[128,1024]{1,0:T(8,128)}, f32[8,128]{1,0:T(8,128)}, bf16[8,1024,128]{2,1,0:T(8,128)(2,1)}) custom-call(s32[16,128]{1,0:T(8,128)} %get-tuple-element.13.tab_s, f32[16,4096]{1,0:T(8,128)} %get-tuple-element.15.grad_ref, bf16[1024,128]{1,0:T(8,128)(2,1)} %get-tuple-element.16.iqr_ref, f32[16,128]{1,0:T(8,128)} %get-tuple-element.17.row_ref, ...), custom_call_target="tpu_custom_call" | custom-call | tf_op jit(solution)/shard_map/give_back/pallas_call | solution.py:782
  177.7 0.0 copy-start
  177.7 0.0 copy-start.1
  177.7 4.8 %scatter.1 = f32[8192,128]{1,0:T(8,128)} custom-call(s32[16,128]{1,0:T(8,128)} %get-tuple-element.21.asked_s, bf16[8,1024,128]{2,1,0:T(8,128)(2,1)} %get-tuple-element.22.kg_ref), custom_call_target="tpu_custom_call" | custom-call | tf_op jit(solution)/shard_map/scatter/pallas_call | solution.py:836
  182.6 0.0 copy-done
  182.6 0.8 copy.13
  183.4 0.0 copy-done.1
  183.4 0.6 copy.14
Async XLA Ops:
  177.7 4.9 %copy-start = (f32[128,1024]{1,0:T(8,128)S(1)}, f32[128,1024]{1,0:T(8,128)}, u32[]{:S(2)}) copy-start(f32[128,1024]{1,0:T(8,128)} %get-tuple-element.26) | copy-start | bytes 1572868
  177.7 5.7 %copy-start.1 = (f32[8,128]{1,0:T(8,128)S(1)}, f32[8,128]{1,0:T(8,128)}, u32[]{:S(2)}) copy-start(f32[8,128]{1,0:T(8,128)} %get-tuple-element.20) | copy-start | bytes 12292

commit v7 on v6

--- a/solution.py
+++ b/solution.py
@@ -203,7 +203,7 @@
         ),
         in_specs=[vm_spec],
         out_specs=(vm_spec, vm_spec),
-        compiler_params=pltpu.CompilerParams(vmem_limit_bytes=60 << 20),
+        compiler_params=pltpu.CompilerParams(vmem_limit_bytes=32 << 20),
     )(sel_t)
 
 
@@ -286,13 +286,19 @@
         s.start()
         sends.append(s)
 
+    other_row = []
     for o in range(1, NH):
         h = lax.rem(me_h + o, NH)
         rows = pl.ds(pl.multiple_of(h * QROWS, QROWS), QROWS)
-        for src, dst, ss, rs in ((iq_hbm.at[rows], iq_ref, i_send, i_recv), (w_hbm, w_ref, w_send, w_recv)):
-            s = remote(src, dst.at[me_h], ss.at[o], rs.at[o], (h, me_c))
+        s = remote(w_hbm, w_ref.at[me_h], w_send.at[o], w_recv.at[o], (h, me_c))
+        s.start()
+        sends.append(s)
+        s = remote(iq_hbm.at[rows], iq_ref.at[me_h], i_send.at[o], i_recv.at[o], (h, me_c))
+        sends.append(s)
+        if o % 2 == 0:
             s.start()
-            sends.append(s)
+        else:
+            other_row.append(s)
     for n in (1, 2, 3):
         send_queries(n)
     own_req.wait()
@@ -334,13 +340,13 @@
     for s in late:
         s.start()
         sends.append(s)
+    for s in other_row:
+        s.start()
     owners = [tab_s[1, me_h * SETB + j] for j in range(SETB)]
 
     own_w.wait()
-    own_iq.wait()
     for o in range(1, NH):
         h = lax.rem(me_h + NH - o, NH)
-        remote(iq_hbm.at[pl.ds(0, QROWS)], iq_ref.at[h], i_send.at[o], i_recv.at[o], (h, me_c)).wait_recv()
         remote(w_hbm, w_ref.at[h], w_send.at[o], w_recv.at[o], (h, me_c)).wait_recv()
     top = sel_ref.shape[0]
     meta_ref[...] = jnp.zeros((128, 128), f32)
@@ -374,6 +380,10 @@
         return carry
 
     lax.fori_loop(0, UNION // 128, mask_tile, 0)
+    own_iq.wait()
+    for o in range(1, NH):
+        h = lax.rem(me_h + NH - o, NH)
+        remote(iq_hbm.at[pl.ds(0, QROWS)], iq_ref.at[h], i_send.at[o], i_recv.at[o], (h, me_c)).wait_recv()
     for h in range(NH):
         for k in range(8):
             iqr_ref[(h * 8 + k) * QROWS : (h * 8 + k + 1) * QROWS, :] = iq_ref[h, :, k * 128 : (k + 1) * 128]

time: 185 us -> 188 us (1.016)
  local copies, waits for them, and re-layouts: 1.39 us -> 3.33 us
    pallas_call x1, Pallas kernels: 109 us -> 113 us  [forward(): pl.pallas_call(forward_kernel, name='forward', out_shape=(jax.ShapeDtypeS...]
    pallas_call x1, Pallas kernels: 66 us -> 64.1 us  [give_back(): pl.pallas_call(return_kernel, name='give_back', out_shape=(jax.ShapeDtype...]
    unnamed x6 -> x12, local copies, waits for them, and re-layouts: 1.39 us -> 3.33 us
where the time goes in v7:
time: 188 us; the launch traced here: 187 us
  Pallas kernels  183 us (97%)
  local copies, waits for them, and re-layouts  3.33 us (2%)
    pallas_call x1, Pallas kernels, forward(): pl.pallas_call(forward_kernel, name='forward', out_shape=(jax.ShapeDtypeS...  113 us
    pallas_call x1, Pallas kernels, give_back(): pl.pallas_call(return_kernel, name='give_back', out_shape=(jax.ShapeDtype...  64.1 us
    pallas_call x1, Pallas kernels, scatter(): pl.pallas_call(scatter_kernel, name='scatter', out_shape=jax.ShapeDtypeSt...  4.85 us

profile of v7, /device:TPU:0, one launch (start us, length us, event | category | flops | bytes accessed | tf_op | source)
XLA Modules:
  0.0 186.8 jit_solution(6862821754630423485)
XLA Ops:
  0.6 0.0 copy-start.1
  0.6 0.7 copy-done.1
  1.4 0.8 plan.1
  2.2 0.0 copy-start
  2.2 0.6 copy-done
  2.8 0.0 copy-start.2
  2.8 0.6 copy-done.2
  3.4 113.1 %forward.1 = (f32[16,4096]{1,0:T(8,128)}, bf16[1024,128]{1,0:T(8,128)(2,1)}, f32[16,128]{1,0:T(8,128)}, s32[16,128]{1,0:T(8,128)}, bf16[8,512,128]{2,1,0:T(8,128)(2,1)}) custom-call(s32[16,128]{1,0:T(8,128)} %copy-done.2, s32[16,8,128]{2,1,0:T(8,128)} %copy-done, s32[32,128]{1,0:T(8,128)} %bitcast.7, s32[1,128]{1,0:T(1,128)} %bitcast.13, f32[1,128]{1,0:T(1,128)} %bitcast.14, ...), custom_call_target="tpu_custom_call" | custom-call | tf_op jit(solution)/shard_map/forward/pallas_call | solution.py:549
  116.5 64.1 %give_back.1 = (f32[128,1024]{1,0:T(8,128)}, f32[8,128]{1,0:T(8,128)}, bf16[8,1024,128]{2,1,0:T(8,128)(2,1)}) custom-call(s32[16,128]{1,0:T(8,128)} %copy-done.2, f32[16,4096]{1,0:T(8,128)} %get-tuple-element.15.grad_ref, bf16[1024,128]{1,0:T(8,128)(2,1)} %get-tuple-element.16.iqr_ref, f32[16,128]{1,0:T(8,128)} %get-tuple-element.17.row_ref, ...), custom_call_target="tpu_custom_call" | custom-call | tf_op jit(solution)/shard_map/give_back/pallas_call | solution.py:792
  180.6 0.0 copy-start.3
  180.6 0.0 copy-start.4
  180.6 4.8 %scatter.1 = f32[8192,128]{1,0:T(8,128)} custom-call(s32[16,128]{1,0:T(8,128)} %get-tuple-element.21.asked_s, bf16[8,1024,128]{2,1,0:T(8,128)(2,1)} %get-tuple-element.22.kg_ref), custom_call_target="tpu_custom_call" | custom-call | tf_op jit(solution)/shard_map/scatter/pallas_call | solution.py:846
  185.4 0.0 copy-done.3
  185.4 0.8 copy.13
  186.2 0.0 copy-done.4
  186.2 0.6 copy.14
Async XLA Ops:
  0.6 0.7 copy-start.1
  2.2 0.6 copy-start
  2.8 0.6 copy-start.2
  180.6 4.9 %copy-start.3 = (f32[128,1024]{1,0:T(8,128)S(1)}, f32[128,1024]{1,0:T(8,128)}, u32[]{:S(2)}) copy-start(f32[128,1024]{1,0:T(8,128)} %get-tuple-element.26) | copy-start | bytes 1572868
  180.6 5.7 %copy-start.4 = (f32[8,128]{1,0:T(8,128)S(1)}, f32[8,128]{1,0:T(8,128)}, u32[]{:S(2)}) copy-start(f32[8,128]{1,0:T(8,128)} %get-tuple-element.20) | copy-start | bytes 12292
